TPU v7x, 256 devices: a whole 4x4x8 slice. The times are simulated.
256 devices in a mesh: dp: 8 (over x, core), tensor: 32 (over y, z).
Axes of the slice: x: 4, y: 4, z: 8, core: 2. Of those that a mesh axis runs over, the one named last changes fastest.
Arguments:
- tokens: bfloat16 [16384, 2048], P(('dp', 'tensor')), may hold values from -6 to 6
- attn_gain: float32 [2048], replicated, may hold values from 0.25 to 1.75
- ffn_gain: float32 [2048], replicated, may hold values from 0.25 to 1.75
- w_attn: bfloat16 [4, 2048, 1024], P(None, None, 'tensor')
- kv_pool: bfloat16 [768, 8, 128, 256], P(('dp', 'tensor'))
- page_table: int32 [8, 72], P('dp'), may hold values from 0 to 95, as said below
- cache_len: int32 [8], P('dp'), may hold values from 2304 to 9216
- routes: int32 [16384, 4], P(('dp', 'tensor')), may hold values from 0 to 63, all different within a row; in each aligned block of 64 rows (0 to 63, 64 to 127, ...) at most 5 rows name the same one
- route_gain: float32 [16384, 4], P(('dp', 'tensor')), may hold values from 0.05 to 0.3
- w_gate_up: bfloat16 [256, 2048, 512], P(('dp', 'tensor')), may hold values from -0.125 to 0.125
- w_down: bfloat16 [256, 256, 2048], P(('dp', 'tensor')), may hold values from -0.1875 to 0.1875
Outputs:
- layer_out: bfloat16 [16384, 2048], P(('dp', 'tensor'))
Inputs may be any that keep to these rules, and one draw needn't show every extreme that they name: `page_table`: each row lists 72 different slots; an entry of value v names slot v % 3 of the device v // 3 along tensor in the request's pool. `routes`: among the 64 tokens of one device no expert is named more than 5 times, and in every draw some expert is named exactly 5 times by one device's tokens. A row names 4 different experts.
All inputs are finite; a program needn't handle non-finite values.
Results may differ from a plain program's by a relative error of at most 0.014.
Values may be sent and summed in bfloat16 or wider, within the bound.
A program may use at most 128 MiB of HBM per device.

v0:
```python
import math

import jax
import jax.numpy as jnp
from jax import lax
from jax.sharding import PartitionSpec as P

HEADS = 8
HD = 128
EXPERTS = 64
TOP = 4


rope_base = 50000.0
norm_eps = 1e-06
very_low = -1e30


def partner(value, axis, apart):
    mask = 2**apart
    pairs = [(source, source ^ mask) for source in range(lax.axis_size(axis))]
    return lax.ppermute(value, axis, pairs)


def rms_scale(rows, gain):
    values = rows.astype(jnp.float32)
    power = jnp.mean(values * values, axis=-1, keepdims=True)
    return (values * lax.rsqrt(power + norm_eps) * gain).astype(jnp.bfloat16)


def rotate(values, positions):
    half = values.shape[-1] // 2
    freq = rope_base ** (-(jnp.arange(half, dtype=jnp.float32) * 2.0) / values.shape[-1])
    angle = positions.astype(jnp.float32)[:, None] * freq[None, :]
    cosine = jnp.cos(angle)
    sine = jnp.sin(angle)
    first = values[:, :half]
    second = values[:, half:]
    return jnp.concatenate([first * cosine - second * sine, second * cosine + first * sine], axis=1)


def expert_pieces(rows, gate_up, down_projected):
    width = down_projected.shape[1]
    both = jnp.einsum("tpacd,pdf->tpacf", rows, gate_up, preferred_element_type=jnp.float32)
    activation = (jax.nn.silu(both[..., :width]) * both[..., width:]).astype(jnp.bfloat16)
    return jnp.einsum(
        "tpacf,pfd->tpacd", activation, down_projected, preferred_element_type=jnp.float32
    )


def local(
    tokens,
    attn_gain,
    ffn_gain,
    w_attn,
    kv_pool,
    page_table,
    cache_len,
    routes,
    route_gain,
    w_gate_up,
    w_down,
):
    tensor_count = lax.axis_size("tensor")
    n_dp = lax.axis_size("dp")
    tok_dev, width = tokens.shape
    split = tensor_count // HEADS
    member = lax.axis_index("tensor")
    head = member // split
    part = member % split
    span = tok_dev * tensor_count
    length = cache_len[0]
    scale = 1.0 / math.sqrt(HD)
    head_cols = w_attn[:3]
    for bit in range(split.bit_length() - 1):
        other = partner(head_cols, "tensor", bit)
        upper = part >> bit & 1 == 1
        head_cols = jnp.where(
            upper,
            jnp.concatenate([other, head_cols], axis=2),
            jnp.concatenate([head_cols, other], axis=2),
        )
    project_w = jnp.concatenate([head_cols[0], head_cols[1], head_cols[2]], axis=1)
    normed = rms_scale(tokens, attn_gain)
    piece = lax.all_gather(normed, "tensor", axis=0, tiled=True)
    positions = length + jnp.arange(piece.shape[0], dtype=jnp.int32)
    product = jnp.dot(piece, project_w, preferred_element_type=jnp.float32)
    query = rotate(product[:, :HD], positions).astype(jnp.bfloat16)
    key_new = rotate(product[:, HD : 2 * HD], positions).astype(jnp.bfloat16)
    mixed = jnp.concatenate([query, key_new, product[:, 2 * HD :].astype(jnp.bfloat16)], axis=1)
    query = mixed[:, :HD]
    new_rows = span // split
    own_new = lax.dynamic_slice_in_dim(mixed, part * new_rows, new_rows, 0)
    slots = kv_pool.shape[0]
    page = kv_pool.shape[2]
    sub = page // split
    sent = kv_pool.reshape(slots, HEADS * split, sub, 2 * HD)
    arrived = lax.all_to_all(sent, "tensor", split_axis=1, concat_axis=0, tiled=True)
    cached = arrived.reshape(tensor_count * slots * sub, 2 * HD)
    table = page_table[0]
    slot_ids = jnp.arange(tensor_count * slots, dtype=jnp.int32)
    hits = table[None, :] == slot_ids[:, None]
    page_of = jnp.sum(
        jnp.where(hits, jnp.arange(table.shape[0], dtype=jnp.int32)[None, :], 0), axis=1
    )
    present = jnp.any(hits, axis=1)
    position = page_of[:, None] * page + part * sub + jnp.arange(sub, dtype=jnp.int32)[None, :]
    live = (present[:, None] & (position < length)).reshape(-1)
    live_all = jnp.concatenate([live, jnp.ones((new_rows,), dtype=bool)])
    keys = jnp.concatenate([cached[:, :HD], own_new[:, HD : 2 * HD]], axis=0)
    values = jnp.concatenate([cached[:, HD:], own_new[:, 2 * HD :]], axis=0)
    q_block = math.gcd(span, 512)
    q_count = span // q_block
    query_blocks = query.reshape(q_count, q_block, HD)

    def block_scores(rows):
        scores = (
            lax.dot_general(
                rows, keys, (((1,), (1,)), ((), ())), preferred_element_type=jnp.float32
            )
            * scale
        )
        return jnp.where(live_all[None, :], scores, very_low)

    column = jnp.arange(HEADS, dtype=jnp.int32)[None, :] == head

    def local_max(rows):
        return jnp.max(block_scores(rows), axis=1)

    local_top = lax.map(local_max, query_blocks).reshape(span)
    top_cols = lax.pmax(
        jnp.where(column, local_top[:, None], very_low).astype(jnp.bfloat16), "tensor"
    ).astype(jnp.float32)
    row_top = jnp.sum(jnp.where(column, top_cols, 0.0), axis=1)

    def weigh_sum(inputs):
        rows, top = inputs
        expo = jnp.exp(block_scores(rows) - top[:, None])
        return (
            jnp.dot(expo.astype(jnp.bfloat16), values, preferred_element_type=jnp.float32),
            jnp.sum(expo, axis=1),
        )

    weighted, sums = lax.map(weigh_sum, (query_blocks, row_top.reshape(q_count, q_block)))
    weighted = weighted.reshape(span, HD)
    total_cols = lax.psum(
        jnp.where(column, sums.reshape(span)[:, None], 0.0).astype(jnp.bfloat16), "tensor"
    ).astype(jnp.float32)
    own_totals = lax.dynamic_slice_in_dim(total_cols, member * tok_dev, tok_dev, 0)
    landed_rows = lax.all_to_all(
        weighted.reshape(span, 1, HD).astype(jnp.bfloat16),
        "tensor",
        split_axis=0,
        concat_axis=1,
        tiled=True,
    ).astype(jnp.float32)
    numer = jnp.sum(landed_rows.reshape(tok_dev, HEADS, split, HD), axis=2)
    merged = (numer / own_totals[..., None]).reshape(tok_dev, HEADS * HD)
    attn = jnp.zeros((tok_dev, width), jnp.float32) + lax.dot_general(
        merged,
        lax.all_gather(w_attn[3], "tensor", axis=1, tiled=True).astype(jnp.float32),
        (((1,), (1,)), ((), ())),
        precision=lax.Precision.HIGHEST,
    )
    hidden = (tokens.astype(jnp.float32) + attn).astype(jnp.bfloat16)
    normed2 = rms_scale(hidden, ffn_gain)
    per_dev = w_gate_up.shape[0]
    exp_dp = EXPERTS // n_dp
    exp_t = exp_dp // per_dev
    quarters = tensor_count // exp_t
    cap = routes.shape[0] * 0 + max(2, tok_dev * TOP * 5 // (4 * EXPERTS))
    flat_expert = routes.reshape(-1)
    onehot = (flat_expert[:, None] == jnp.arange(EXPERTS, dtype=jnp.int32)[None, :]).astype(
        jnp.int32
    )
    rank = jnp.sum(jnp.cumsum(onehot, axis=0) * onehot, axis=1) - 1
    slot_id = (flat_expert % exp_dp * n_dp + flat_expert // exp_dp) * cap + rank
    total_slots = exp_dp * n_dp * cap
    place = (slot_id[:, None] == jnp.arange(total_slots, dtype=jnp.int32)[None, :]).astype(
        jnp.float32
    )
    token_of = (
        jnp.arange(tok_dev * TOP, dtype=jnp.int32)[:, None] // TOP
        == jnp.arange(tok_dev, dtype=jnp.int32)[None, :]
    ).astype(jnp.float32)
    dispatch = jnp.dot(place.T, token_of, precision=lax.Precision.HIGHEST).astype(jnp.bfloat16)
    combine = jnp.dot(
        token_of.T, place * route_gain.reshape(-1)[:, None], precision=lax.Precision.HIGHEST
    )
    buffer = jnp.dot(dispatch, normed2, preferred_element_type=jnp.float32).astype(jnp.bfloat16)
    buffer = buffer.reshape(exp_dp, n_dp, cap, width)
    landed = lax.all_to_all(buffer, "dp", split_axis=1, concat_axis=1, tiled=True)
    grouped = landed.reshape(exp_t, per_dev, n_dp, cap, width)
    copies = jnp.broadcast_to(grouped[None], (quarters, exp_t, per_dev, n_dp, cap, width)).reshape(
        tensor_count, per_dev, n_dp, cap, width
    )
    partial_out = expert_pieces(
        lax.all_to_all(copies, "tensor", split_axis=0, concat_axis=0, tiled=True), w_gate_up, w_down
    ).astype(jnp.bfloat16)
    returned = lax.all_to_all(partial_out, "tensor", split_axis=0, concat_axis=0, tiled=True)
    summed = jnp.sum(
        returned.astype(jnp.float32).reshape(quarters, exp_dp, n_dp, cap, width), axis=0
    )
    output_rows = lax.all_to_all(
        summed.astype(jnp.bfloat16), "dp", split_axis=1, concat_axis=1, tiled=True
    ).astype(summed.dtype)
    moe = jnp.dot(combine, output_rows.reshape(total_slots, width), precision=lax.Precision.HIGHEST)
    return (hidden.astype(jnp.float32) + moe).astype(jnp.bfloat16)


def solution(mesh):
    placed = (
        P(("dp", "tensor"), None),
        P(),
        P(),
        P(None, None, "tensor"),
        P(("dp", "tensor"), None, None, None),
        P("dp", None),
        P("dp"),
        P(("dp", "tensor"), None),
        P(("dp", "tensor"), None),
        P(("dp", "tensor"), None, None),
        P(("dp", "tensor"), None, None),
    )
    return jax.shard_map(
        local, mesh=mesh, in_specs=placed, out_specs=P(("dp", "tensor"), None), check_vma=False
    )
```

profile of v0, /device:TPU:1, one launch (start us, length us, event | category | flops | bytes accessed | tf_op | source)
XLA Modules:
  0.0 833.4 jit_solution(3819508705786121760)
XLA Ops:
  9.6 2.7 copy.60
  12.3 12.3 %all-to-all-start = ((bf16[3,32,32,256]{3,2,0,1:T(8,128)(2,1)}), bf16[3,32,32,256]{3,2,0,1:T(8,128)(2,1)}, u32[]{:S(2)}, u32[]{:S(2)}) async-start(bf16[3,32,32,256]{3,2,0,1:T(8,128)(2,1)} %copy.60), calls=%async_computation | async-start | bytes 3145728 | tf_op jit(solution)/shard_map/all_to_all | solution.py:98
  28.0 50.1 %collective-permute-done = bf16[3,2048,32]{1,2,0:T(8,128)(2,1)} collective-permute-done((bf16[3,2048,32]{1,2,0:T(8,128)(2,1)S(1)}, bf16[3,2048,32]{1,2,0:T(8,128)(2,1)}, u32[]{:S(2)}, u32[]{:S(2)}) %collective-permute-start) | collective-permute-done | bytes 393248 | tf_op jit(solution)/shard_map/ppermute | solution.py:22
  83.1 49.2 %collective-permute-done.1 = bf16[3,2048,64]{1,2,0:T(8,128)(2,1)} collective-permute-done((bf16[3,2048,64]{1,2,0:T(8,128)(2,1)S(1)}, bf16[3,2048,64]{1,2,0:T(8,128)(2,1)}, u32[]{:S(2)}, u32[]{:S(2)}) %collective-permute-start.1) | collective-permute-done | bytes 786464 | tf_op jit(solution)/shard_map/ppermute | solution.py:22
  137.8 16.5 %all-gather.4.cloned.1.call-done = bf16[2048,2048]{1,0:T(8,128)(2,1)} async-done(((bf16[64,2048]{1,0:T(8,128)(2,1)}), bf16[2048,2048]{1,0:T(8,128)(2,1)}) %all-gather.4.cloned.1.call-update) | async-done | bytes 8388624 | tf_op jit(solution)/shard_map/all_gather | solution.py:85
  154.3 6.1 fusion.34
  160.5 2.9 constant_dynamic-update-slice_fusion.1
  163.4 2.9 constant_dynamic-update-slice_fusion
  178.1 10.1 %while.22 = (s32[]{:T(128)}, bf16[4,512]{1,0:T(4,128)(2,1)S(1)}, pred[3584]{0:T(1024)(128)(4,1)S(1)}, bf16[4,512,128]{2,1,0:T(8,128)(2,1)}, bf16[3584,128]{1,0:T(8,128)(2,1)}, /*index=5*/s32[]{:T(128)}, s32[]{:T(128)}) while((s32[]{:T(128)}, bf16[4,512]{1,0:T(4,128)(2,1)S(1)}, pred[3584]{0:T(1024)(128)(4,1)S(1)}, ...), condition=%wide.region_5.6_spmd, body=%wide.region_3.5_spmd.sunk | while | flops 475266560 | bytes 1058897 | solution.py:130
  188.3 115.9 %pmax.7 = bf16[2048,8]{0,1:T(8,128)(2,1)S(1)} all-reduce(bf16[2048,8]{0,1:T(8,128)(2,1)S(1)} %select_convert_fusion.1), channel_id=1, replica_groups=mesh['dp'=8,'tensor'=32] {'tensor'}, use_global_device_ids=true, to_apply=%region_6.7 | all-reduce | flops 16384 | bytes 65536 | tf_op jit(solution)/shard_map/pmax | solution.py:131
  305.6 21.5 %while.23 = (s32[]{:T(128)}, bf16[4,512,128]{2,1,0:T(8,128)(2,1)}, bf16[4,512]{1,0:T(4,128)(2,1)S(1)}, pred[3584]{0:T(1024)(128)(4,1)}, bf16[4,512,128]{2,1,0:T(...) while((s32[]{:T(128)}, bf16[4,512,128]{2,1,0:T(8,128)(2,1)}, ...), condition=%wide.region_10.11_spmd, body=%wide.region_8.10_spmd.sunk | while | flops 948698624 | bytes 13779625 | solution.py:144
  305.6 3.3 fusion.113
  311.0 3.3 fusion.113
  316.3 3.4 fusion.113
  321.7 3.3 fusion.113
  330.5 3.9 all-to-all-start.1
  334.9 115.8 %psum.7 = bf16[2048,8]{0,1:T(8,128)(2,1)S(1)} all-reduce(bf16[2048,8]{0,1:T(8,128)(2,1)S(1)} %select_convert_fusion), channel_id=1, replica_groups=mesh['dp'=8,'tensor'=32] {'tensor'}, use_global_device_ids=true, to_apply=%region_12.13 | all-reduce | flops 16384 | bytes 65536 | tf_op jit(solution)/shard_map/psum | solution.py:146
  455.5 4.8 multiply_reduce_fusion
  465.8 77.6 %all_to_all.44 = bf16[8,8,5,2048]{3,0,2,1:T(8,128)(2,1)S(1)} all-to-all(bf16[8,8,5,2048]{3,0,2,1:T(8,128)(2,1)S(1)} %copy.69), channel_id=1, replica_groups=mesh['dp'=8,'tensor'=32] {'dp'}, dimensions={1} | all-to-all | bytes 2621440 | tf_op jit(solution)/shard_map/all_to_all | solution.py:192
  544.8 117.5 %all_to_all.45 = bf16[32,1,8,5,2048]{4,2,3,1,0:T(8,128)(2,1)S(1)} all-to-all(bf16[32,1,8,5,2048]{4,2,3,1,0:T(8,128)(2,1)S(1)} %bitcast.148), channel_id=1, replica_groups=mesh['dp'=8,'tensor'=32] {'tensor'}, dimensions={0} | all-to-all | bytes 10485760 | tf_op jit(solution)/shard_map/all_to_all | solution.py:198
  662.4 2.9 fusion.29
  666.8 123.0 %all_to_all.46 = bf16[32,1,8,5,2048]{4,2,3,1,0:T(8,128)(2,1)S(1)} all-to-all(bf16[32,1,8,5,2048]{4,2,3,1,0:T(8,128)(2,1)S(1)} %convert_bitcast_fusion), channel_id=1, replica_groups=mesh['dp'=8,'tensor'=32] {'tensor'}, dimensions={0} | all-to-all | bytes 10485760 | tf_op jit(solution)/shard_map/all_to_all | solution.py:200
  792.6 8.6 %all-to-all-start.5 = ((bf16[8,8,5,2048]{3,0,2,1:T(8,128)(2,1)}), bf16[8,8,5,2048]{3,0,2,1:T(8,128)(2,1)S(1)}, u32[]{:S(2)}, u32[]{:S(2)}) async-start(bf16[8,8,5,2048]{3,0,2,1:T(8,128)(2,1)} %copy.72), calls=%async_computation.5 | async-start | bytes 2621440 | tf_op jit(solution)/shard_map/all_to_all | solution.py:204
  801.9 17.3 %all-to-all-done.5 = bf16[8,8,5,2048]{3,0,2,1:T(8,128)(2,1)S(1)} async-done(((bf16[8,8,5,2048]{3,0,2,1:T(8,128)(2,1)}), bf16[8,8,5,2048]{3,0,2,1:T(8,128)(2,1)S(1)}, u32[]{:S(2)}, u32[]{:S(2)}) %all-to-all-start.5) | async-done | bytes 1310752 | tf_op jit(solution)/shard_map/all_to_all | solution.py:204
  (148 shorter events, 75.3 us)
Async XLA Ops:
  6.5 655.8 %copy-start = (bf16[1,2048,512]{2,1,0:T(8,128)(2,1)S(1)}, bf16[1,2048,512]{2,1,0:T(8,128)(2,1)}, u32[]{:S(2)}) copy-start(bf16[1,2048,512]{2,1,0:T(8,128)(2,1)} %param.24) | copy-start | bytes 6291460
  6.5 147.8 %all-gather.4.cloned.1.call-start = ((), (), s32[]{:S(2)}) async-start(), calls=%async_computation.6 | async-start | bytes 8650752 | tf_op jit(solution)/shard_map/all_gather | solution.py:85
  12.3 12.3 %copy-start.4 = (bf16[4,2048,32]{1,2,0:T(8,128)(2,1)S(1)}, bf16[4,2048,32]{1,2,0:T(8,128)(2,1)}, u32[]{:S(2)}) copy-start(bf16[4,2048,32]{1,2,0:T(8,128)(2,1)} %param.18) | copy-start | bytes 1572868
  12.3 14.3 %copy-start.17 = (s32[1,72]{1,0:T(1,128)S(1)}, s32[1,72]{1,0:T(1,128)}, u32[]{:S(2)}) copy-start(s32[1,72]{1,0:T(1,128)} %param.20) | copy-start | bytes 868
  12.3 14.5 %copy-start.14 = (s32[64,4]{0,1:T(4,128)S(1)}, s32[64,4]{0,1:T(4,128)}, u32[]{:S(2)}) copy-start(s32[64,4]{0,1:T(4,128)} %param.22) | copy-start | bytes 3076
  12.3 123.2 %all-to-all-start = ((bf16[3,32,32,256]{3,2,0,1:T(8,128)(2,1)}), bf16[3,32,32,256]{3,2,0,1:T(8,128)(2,1)}, u32[]{:S(2)}, u32[]{:S(2)}) async-start(bf16[3,32,32,256]{3,2,0,1:T(8,128)(2,1)} %copy.60), calls=%async_computation | async-start | bytes 3145728 | tf_op jit(solution)/shard_map/all_to_all | solution.py:98
  24.6 431.0 %all-gather.6.cloned.1.call-start = ((), (), s32[]{:S(2)}) async-start(), calls=%async_computation.7 | async-start | bytes 4325376 | tf_op jit(solution)/shard_map/all_gather | solution.py:161
  24.7 53.4 %collective-permute-start = (bf16[3,2048,32]{1,2,0:T(8,128)(2,1)S(1)}, bf16[3,2048,32]{1,2,0:T(8,128)(2,1)}, u32[]{:S(2)}, u32[]{:S(2)}) collective-permute-start(bf16[3,2048,32]{1,2,0:T(8,128)(2,1)S(1)} %slice.61), channel_id=1, source_target_pairs={{0,1},{1,0},{2,3},{3,2},{4,5},{5,4},{6,7},{7,6},{8,9},{9,8},{10,11... | collective-permute-start | bytes 1179656 | tf_op jit(solution)/shard_map/ppermute | solution.py:22
  27.1 105.2 %copy-start.7 = (s32[256]{0:T(256)}, s32[256]{0:T(256)S(1)}, u32[]{:S(2)}) copy-start(s32[256]{0:T(256)S(1)} %reshape.245) | copy-start | bytes 3076
  79.6 52.7 %collective-permute-start.1 = (bf16[3,2048,64]{1,2,0:T(8,128)(2,1)S(1)}, bf16[3,2048,64]{1,2,0:T(8,128)(2,1)}, u32[]{:S(2)}, u32[]{:S(2)}) collective-permute-start(bf16[3,2048,64]{1,2,0:T(8,128)(2,1)S(1)} %maximum_select_fusion.1), channel_id=1, source_target_pairs={{0,2},{1,3},{2,0},{3,1},{4,6},{5,7},{6,4},{7,5},{8,10},{9,11},{10,... | collective-permute-start | bytes 2359304 | tf_op jit(solution)/shard_map/ppermute | solution.py:22
  82.4 221.8 %copy-start.10 = (pred[8]{0:T(512)(128)(4,1)}, pred[8]{0:T(512)(128)(4,1)S(1)}, u32[]{:S(2)}) copy-start(pred[8]{0:T(512)(128)(4,1)S(1)} %iota_compare_fusion.9) | copy-start | bytes 28
  178.1 126.2 %copy-start.3 = (bf16[512,128]{0,1:T(8,128)(2,1)S(1)}, bf16[512,128]{0,1:T(8,128)(2,1)}, u32[]{:S(2)}) copy-start(bf16[512,128]{0,1:T(8,128)(2,1)} %get-tuple-element.112) | copy-start | bytes 393220
  188.2 116.0 %copy-start.13 = (pred[3584]{0:T(1024)(128)(4,1)}, pred[3584]{0:T(1024)(128)(4,1)S(1)}, u32[]{:S(2)}) copy-start(pred[3584]{0:T(1024)(128)(4,1)S(1)} %get-tuple-element.275) | copy-start | bytes 10756
  305.6 3.4 copy-start.5
  311.0 3.3 copy-start.5
  316.3 3.4 copy-start.5
  321.7 3.3 copy-start.5
  327.0 7.4 copy-start.8
  327.1 7.4 copy-start.12
  327.1 7.7 copy-start.11
  330.5 120.2 %all-to-all-start.1 = ((bf16[32,2,4096]{2,1,0:T(2,128)(2,1)}), bf16[32,2,4096]{2,1,0:T(2,128)(2,1)S(1)}, u32[]{:S(2)}, u32[]{:S(2)}) async-start(bf16[32,2,4096]{2,1,0:T(2,128)(2,1)} %reshape.261), calls=%async_computation.1 | async-start | bytes 1048576 | tf_op jit(solution)/shard_map/all_to_all | solution.py:150
  455.5 5.6 copy-start.9
  792.6 8.7 %copy-start.15 = (f32[64,4]{0,1:T(4,128)S(1)}, f32[64,4]{0,1:T(4,128)}, u32[]{:S(2)}) copy-start(f32[64,4]{0,1:T(4,128)} %param.23) | copy-start | bytes 3076
  792.6 26.6 %all-to-all-start.5 = ((bf16[8,8,5,2048]{3,0,2,1:T(8,128)(2,1)}), bf16[8,8,5,2048]{3,0,2,1:T(8,128)(2,1)S(1)}, u32[]{:S(2)}, u32[]{:S(2)}) async-start(bf16[8,8,5,2048]{3,0,2,1:T(8,128)(2,1)} %copy.72), calls=%async_computation.5 | async-start | bytes 2621440 | tf_op jit(solution)/shard_map/all_to_all | solution.py:204
  (7 other events, 10.0 us)
Sparse Core Ops, SparseCore 0:
  10.0 144.3 all-gather.3
  156.9 81.2 all-gather.5
where the time goes:
time: 835 us; the launch traced here: 833 us
  blocking collectives  550 us (66%)
  waiting for transfers between devices  133 us (16%)
  matrix products  47.3 us (6%)
  local copies, waits for them, and re-layouts  31.3 us (4%)
  other arithmetic  29.2 us (3%)
  starting transfers between devices  28 us (3%)
  between operations  14.5 us (2%)
    all_to_all x1, blocking collectives, local(): lax.all_to_all(partial_out, 'tensor', split_axis=0, concat_axis=0, tiled=...  123 us
    all_to_all x1, blocking collectives, local(): lax.all_to_all(copies, 'tensor', split_axis=0, concat_axis=0, tiled=True)  118 us
    pmax x1, blocking collectives, local(): lax.pmax(jnp.where(column, local_top[:, None], very_low).astype(jnp.bfloa...  116 us
    psum x1, blocking collectives, local(): lax.psum(jnp.where(column, sums.reshape(span)[:, None], 0.0).astype(jnp.b...  116 us
    ppermute x2, waiting for transfers between devices, partner(): return lax.ppermute(value, axis, pairs)  99.3 us
    all_to_all x1, blocking collectives, local(): lax.all_to_all(buffer, 'dp', split_axis=1, concat_axis=1, tiled=True)  77.6 us
    dot_general x8, matrix products, block_scores(): lax.dot_general(rows, keys, (((1,), (1,)), ((), ())), preferred_element_t...  23.3 us
    all_to_all x1, waiting for transfers between devices, local(): lax.all_to_all(summed.astype(jnp.bfloat16), 'dp', split_axis=1, concat_ax...  17.3 us
  transfers between devices with their start and end apart: 7, of which 4 were waited for; matrix products, arithmetic and copies ran while one was open for 9% of the time, Pallas kernels for 0%

commit v1 on v0

v1 whole, which is shorter than its diff:
```python
import functools
import math

import jax
import jax.numpy as jnp
from jax import lax
from jax.experimental import pallas as pl
from jax.experimental.pallas import tpu as pltpu
from jax.sharding import Mesh, PartitionSpec as P

HEADS = 8
HD = 128
EXPERTS = 64
TOP = 4

rope_base = 50000.0
norm_eps = 1e-06
very_low = -1e30

GROUP = ("y", "zh", "zl")
EXPERT_AXES = ("dp", "zh", "zl")


def rms_scale(rows, gain):
    values = rows.astype(jnp.float32)
    power = jnp.mean(values * values, axis=-1, keepdims=True)
    return (values * lax.rsqrt(power + norm_eps) * gain).astype(jnp.bfloat16)


def rotate(values, positions):
    half = values.shape[-1] // 2
    freq = rope_base ** (-(jnp.arange(half, dtype=jnp.float32) * 2.0) / values.shape[-1])
    angle = positions.astype(jnp.float32)[:, None] * freq[None, :]
    cosine = jnp.cos(angle)
    sine = jnp.sin(angle)
    first = values[:, :half]
    second = values[:, half:]
    return jnp.concatenate([first * cosine - second * sine, second * cosine + first * sine], axis=1)


def attend_kernel(q_ref, kv_ref, new_ref, bias_ref, out_ref):
    q = q_ref[...]
    scale = 1.0 / math.sqrt(HD)
    old = kv_ref.shape[0]
    nt = (((1,), (1,)), ((), ()))
    s_old = lax.dot_general(q, kv_ref[:, :HD], nt, preferred_element_type=jnp.float32) * scale
    s_old = jnp.where(bias_ref[...] < 0.0, very_low, s_old)
    s_new = lax.dot_general(q, new_ref[:, :HD], nt, preferred_element_type=jnp.float32) * scale
    top = jnp.maximum(
        jnp.max(s_old, axis=1, keepdims=True), jnp.max(s_new, axis=1, keepdims=True)
    )
    top = top.astype(jnp.bfloat16).astype(jnp.float32)
    e_old = jnp.exp(s_old - top)
    e_new = jnp.exp(s_new - top)
    total = jnp.sum(e_old, axis=1, keepdims=True) + jnp.sum(e_new, axis=1, keepdims=True)
    mixed = jnp.dot(
        e_old.astype(jnp.bfloat16), kv_ref[:, HD:], preferred_element_type=jnp.float32
    ) + jnp.dot(e_new.astype(jnp.bfloat16), new_ref[:, HD:], preferred_element_type=jnp.float32)
    out_ref[:, :HD] = mixed.astype(jnp.bfloat16)
    coarse = total.astype(jnp.bfloat16).astype(jnp.float32)
    lane = lax.broadcasted_iota(jnp.int32, (q.shape[0], HD), 1)
    stats = jnp.where(lane == 0, top, jnp.where(lane == 1, coarse, total - coarse))
    out_ref[:, HD:] = stats.astype(jnp.bfloat16)


def attend(query, cached, fresh, bias):
    rows = query.shape[0]
    block = math.gcd(rows, 256)
    old, new = cached.shape[0], fresh.shape[0]
    return pl.pallas_call(
        attend_kernel,
        grid=(rows // block,),
        out_shape=jax.ShapeDtypeStruct((rows, 2 * HD), jnp.bfloat16),
        in_specs=[
            pl.BlockSpec((block, HD), lambda i: (i, 0)),
            pl.BlockSpec((old, 2 * HD), lambda i: (0, 0)),
            pl.BlockSpec((new, 2 * HD), lambda i: (0, 0)),
            pl.BlockSpec((1, old), lambda i: (0, 0)),
        ],
        out_specs=pl.BlockSpec((block, 2 * HD), lambda i: (i, 0)),
        cost_estimate=pl.CostEstimate(
            flops=4 * rows * (old + new) * HD,
            bytes_accessed=6 * (rows + old + new) * HD,
            transcendentals=rows * (old + new),
        ),
    )(query, cached, fresh, bias)


def local(
    tokens,
    attn_gain,
    ffn_gain,
    w_attn,
    kv_pool,
    page_table,
    cache_len,
    routes,
    route_gain,
    w_gate_up,
    w_down,
):
    group = lax.axis_size("y") * lax.axis_size("zh") * lax.axis_size("zl")
    split = lax.axis_size("zl")
    part = lax.axis_index("zl")
    tok_dev, width = tokens.shape
    span = tok_dev * group
    length = cache_len[0]

    sent_w = jnp.transpose(w_attn[:3], (0, 2, 1))
    head_w = lax.all_gather(sent_w, "zl", axis=1, tiled=True)
    project_w = head_w.reshape(3 * HD, width)
    normed = rms_scale(tokens, attn_gain)
    piece = lax.all_gather(normed, ("y", "zh"), axis=0, tiled=True)

    slots = kv_pool.shape[0]
    page = kv_pool.shape[2]
    sub = page // split
    sent = kv_pool.reshape(slots, HEADS * split, sub, 2 * HD)
    arrived = lax.all_to_all(sent, GROUP, split_axis=1, concat_axis=0, tiled=True)
    cached = arrived.reshape(group * slots * sub, 2 * HD)

    out_w = lax.all_gather(jnp.transpose(w_attn[3], (1, 0)), GROUP, axis=0, tiled=True)

    place_of = jnp.arange(piece.shape[0], dtype=jnp.int32)
    positions = length + (place_of // tok_dev * split + part) * tok_dev + place_of % tok_dev
    product = lax.dot_general(
        piece, project_w, (((1,), (1,)), ((), ())), preferred_element_type=jnp.float32
    )
    query = rotate(product[:, :HD], positions).astype(jnp.bfloat16)
    key_new = rotate(product[:, HD : 2 * HD], positions).astype(jnp.bfloat16)
    fresh = jnp.concatenate([key_new, product[:, 2 * HD :].astype(jnp.bfloat16)], axis=1)

    query = query.reshape(1, group // split, tok_dev, HD)
    query = jnp.broadcast_to(query, (split,) + query.shape[1:])
    query = lax.all_to_all(query, "zl", split_axis=0, concat_axis=0, tiled=True)
    query = jnp.transpose(query, (1, 0, 2, 3)).reshape(span, HD)

    table = page_table[0]
    slot_ids = jnp.arange(group * slots, dtype=jnp.int32)
    hits = table[None, :] == slot_ids[:, None]
    page_of = jnp.sum(
        jnp.where(hits, jnp.arange(table.shape[0], dtype=jnp.int32)[None, :], 0), axis=1
    )
    present = jnp.any(hits, axis=1)
    position = page_of[:, None] * page + part * sub + jnp.arange(sub, dtype=jnp.int32)[None, :]
    live = (present[:, None] & (position < length)).reshape(1, -1)
    bias = jnp.where(live, 0.0, very_low).astype(jnp.float32)

    packed = attend(query, cached, fresh, bias)
    landed_rows = lax.all_to_all(
        packed.reshape(group, tok_dev, 2 * HD), GROUP, split_axis=0, concat_axis=0, tiled=True
    ).astype(jnp.float32).reshape(HEADS, split, tok_dev, 2 * HD)
    tops = landed_rows[..., HD]
    weight = jnp.exp(tops - jnp.max(tops, axis=1, keepdims=True))
    totals = jnp.sum(weight * (landed_rows[..., HD + 1] + landed_rows[..., HD + 2]), axis=1)
    numer = jnp.sum(weight[..., None] * landed_rows[..., :HD], axis=1)
    merged = numer / totals[..., None]
    merged = jnp.transpose(merged, (1, 0, 2)).reshape(tok_dev, HEADS * HD)
    attn = jnp.dot(merged, out_w.astype(jnp.float32), precision=lax.Precision.HIGHEST)
    hidden = (tokens.astype(jnp.float32) + attn).astype(jnp.bfloat16)
    normed2 = rms_scale(hidden, ffn_gain)

    gate_up = lax.all_gather(w_gate_up, "y", axis=0, tiled=True)
    down = lax.all_gather(w_down, "y", axis=0, tiled=True)

    cap = max(2, tok_dev * TOP * 5 // (4 * EXPERTS))
    flat_expert = routes.reshape(-1)
    onehot = (flat_expert[:, None] == jnp.arange(EXPERTS, dtype=jnp.int32)[None, :]).astype(
        jnp.int32
    )
    rank = jnp.sum(jnp.cumsum(onehot, axis=0) * onehot, axis=1) - 1
    slot_id = flat_expert * cap + rank
    total_slots = EXPERTS * cap
    place = (slot_id[:, None] == jnp.arange(total_slots, dtype=jnp.int32)[None, :]).astype(
        jnp.float32
    )
    token_of = (
        jnp.arange(tok_dev * TOP, dtype=jnp.int32)[:, None] // TOP
        == jnp.arange(tok_dev, dtype=jnp.int32)[None, :]
    ).astype(jnp.float32)
    dispatch = jnp.dot(place.T, token_of, precision=lax.Precision.HIGHEST).astype(jnp.bfloat16)
    combine = jnp.dot(
        token_of.T, place * route_gain.reshape(-1)[:, None], precision=lax.Precision.HIGHEST
    )
    buffer = jnp.dot(dispatch, normed2, preferred_element_type=jnp.float32).astype(jnp.bfloat16)
    landed = lax.all_to_all(
        buffer.reshape(EXPERTS, cap, width), EXPERT_AXES, split_axis=0, concat_axis=0, tiled=True
    ).reshape(total_slots, width)

    units = w_down.shape[1]
    both = jnp.einsum("rd,qdf->qrf", landed, gate_up, preferred_element_type=jnp.float32)
    activation = (jax.nn.silu(both[..., :units]) * both[..., units:]).astype(jnp.bfloat16)
    summed = jnp.einsum("qrf,qfd->rd", activation, down, preferred_element_type=jnp.float32)
    output_rows = lax.all_to_all(
        summed.astype(jnp.bfloat16).reshape(EXPERTS, cap, width),
        EXPERT_AXES,
        split_axis=0,
        concat_axis=0,
        tiled=True,
    ).reshape(total_slots, width)
    moe = jnp.dot(combine, output_rows.astype(jnp.float32), precision=lax.Precision.HIGHEST)
    return (hidden.astype(jnp.float32) + moe).astype(jnp.bfloat16)


def solution(mesh):
    n_dp, n_tensor = mesh.devices.shape
    inner = Mesh(
        mesh.devices.reshape(n_dp, n_tensor // 8, 2, 4), ("dp", "y", "zh", "zl")
    )
    everywhere = ("dp",) + GROUP
    placed = (
        P(everywhere, None),
        P(),
        P(),
        P(None, None, GROUP),
        P(everywhere, None, None, None),
        P("dp", None),
        P("dp"),
        P(everywhere, None),
        P(everywhere, None),
        P(everywhere, None, None),
        P(everywhere, None, None),
    )
    return jax.shard_map(
        local, mesh=inner, in_specs=placed, out_specs=P(everywhere, None), check_vma=False
    )
```

time: 835 us -> 448 us (0.54)
  blocking collectives: 550 us -> 63.7 us
  waiting for transfers between devices: 133 us -> 275 us
  matrix products: 47.3 us -> 24.7 us
  other arithmetic: 29.2 us -> 8.49 us
  Pallas kernels: 0 us -> 17 us
  local copies, waits for them, and re-layouts: 31.3 us -> 17.3 us
    all_to_all x3 -> x1, blocking collectives: 318 us -> 63.7 us  [local(): lax.all_to_all(buffer.reshape(EXPERTS, cap, width), EXPERT_AXES, split_ax...]
    all_gather x2 -> x5, waiting for transfers between devices: 16.5 us -> 147 us  [the longest x1 77.3 us: local(): piece = lax.all_gather(normed, ('y', 'zh'), axis=0, tiled=True)]
    pmax x1 -> x0, blocking collectives: 116 us -> none  [local(): lax.pmax(jnp.where(column, local_top[:, None], very_low).astype(jnp.bfloa...]
    psum x1 -> x0, blocking collectives: 116 us -> none  [local(): lax.psum(jnp.where(column, sums.reshape(span)[:, None], 0.0).astype(jnp.b...]
    all_to_all x3 -> x4, waiting for transfers between devices: 17.3 us -> 127 us  [the longest x1 51.2 us: local(): lax.all_to_all(summed.astype(jnp.bfloat16).reshape(EXPERTS, cap, width),...]
    ppermute x2 -> x0, waiting for transfers between devices: 99.3 us -> none  [partner(): return lax.ppermute(value, axis, pairs)]
    dot_general x17 -> x5, matrix products: 46 us -> 23.4 us  [the longest x1 8.22 us: local(): jnp.einsum('rd,qdf->qrf', landed, gate_up, preferred_element_type=jnp.flo...]
    pallas_call x0 -> x1, Pallas kernels: none -> 17 us  [attend(): pl.pallas_call(attend_kernel, grid=(rows // block,), out_shape=jax.ShapeD...]
  transfers between devices with their start and end apart: 7 -> 9, of which waited for: 4 -> 7; matrix products, arithmetic and copies ran while one was open for 9% -> 8% of each run, Pallas kernels for 0% -> 4%
where the time goes in v1:
time: 448 us; the launch traced here: 447 us
  waiting for transfers between devices  275 us (61%)
  blocking collectives  63.7 us (14%)
  starting transfers between devices  26.9 us (6%)
  matrix products  24.7 us (6%)
  local copies, waits for them, and re-layouts  17.3 us (4%)
  Pallas kernels  17 us (4%)
  between operations  14.1 us (3%)
  other arithmetic  8.49 us (2%)
    all_gather x1, waiting for transfers between devices, local(): piece = lax.all_gather(normed, ('y', 'zh'), axis=0, tiled=True)  77.3 us
    all_to_all x1, blocking collectives, local(): lax.all_to_all(buffer.reshape(EXPERTS, cap, width), EXPERT_AXES, split_ax...  63.7 us
    all_to_all x1, waiting for transfers between devices, local(): lax.all_to_all(summed.astype(jnp.bfloat16).reshape(EXPERTS, cap, width),...  51.2 us
    all_gather x1, waiting for transfers between devices, local(): head_w = lax.all_gather(sent_w, 'zl', axis=1, tiled=True)  40.2 us
    all_to_all x1, waiting for transfers between devices, local(): lax.all_to_all(sent, GROUP, split_axis=1, concat_axis=0, tiled=True)  39.4 us
    all_gather x1, waiting for transfers between devices, local(): down = lax.all_gather(w_down, 'y', axis=0, tiled=True)  29.5 us
    all_to_all x1, waiting for transfers between devices, local(): lax.all_to_all(packed.reshape(group, tok_dev, 2 * HD), GROUP, split_axis=...  22.1 us
    pallas_call x1, Pallas kernels, attend(): pl.pallas_call(attend_kernel, grid=(rows // block,), out_shape=jax.ShapeD...  17 us
  transfers between devices with their start and end apart: 9, of which 7 were waited for; matrix products, arithmetic and copies ran while one was open for 8% of the time, Pallas kernels for 4%

profile of v1, /device:TPU:1, one launch (start us, length us, event | category | flops | bytes accessed | tf_op | source)
XLA Modules:
  0.0 447.0 jit_solution(8588779077430872405)
XLA Ops:
  6.5 1.8 slice_bitcast_fusion
  9.5 1.8 fusion.10
  14.2 40.2 %all-gather.8.cloned.1.call-done = bf16[3,128,2048]{2,1,0:T(8,128)(2,1)} async-done(((bf16[3,32,2048]{2,1,0:T(8,128)(2,1)}), bf16[3,128,2048]{2,1,0:T(8,128)(2,1)}) %all-gather.8.cloned.1.call-update) | async-done | bytes 1572880 | tf_op jit(solution)/shard_map/all_gather | solution.py:110
  54.4 77.3 %all-gather.6.cloned.1.call-done = bf16[512,2048]{1,0:T(8,128)(2,1)} async-done(((bf16[64,2048]{1,0:T(8,128)(2,1)}), bf16[512,2048]{1,0:T(8,128)(2,1)}) %all-gather.6.cloned.1.call-update) | async-done | bytes 2097168 | tf_op jit(solution)/shard_map/all_gather | solution.py:113
  131.7 3.3 fusion.63
  137.3 3.5 all-to-all-start
  142.1 14.1 %all-to-all-done = bf16[4,8,64,128]{3,2,1,0:T(8,128)(2,1)S(1)} async-done(((bf16[4,8,64,128]{3,2,1,0:T(8,128)(2,1)}), bf16[4,8,64,128]{3,2,1,0:T(8,128)(2,1)S(1)}, u32[]{:S(2)}, u32[]{:S(2)}) %all-to-all-start) | async-done | bytes 524320 | tf_op jit(solution)/shard_map/all_to_all | solution.py:135
  156.2 4.0 all-to-all-start.1
  162.9 39.4 %all-to-all-done.1 = bf16[3,32,32,256]{3,2,0,1:T(8,128)(2,1)S(1)} async-done(((bf16[3,32,32,256]{3,2,0,1:T(8,128)(2,1)}), bf16[3,32,32,256]{3,2,0,1:T(8,128)(2,1)S(1)}, u32[]{:S(2)}, u32[]{:S(2)}) %all-to-all-start.1) | async-done | bytes 1572896 | tf_op jit(solution)/shard_map/all_to_all | solution.py:119
  203.5 17.0 %shard_map.109 = bf16[2048,256]{1,0:T(8,128)(2,1)} custom-call(bf16[2048,128]{1,0:T(8,128)(2,1)} %bitcast.89, bf16[3072,256]{1,0:T(8,128)(2,1)} %bitcast.85, bf16[512,256]{1,0:T(8,128)(2,1)} %pad_maximum_fusion.new_ref, f32[1,3072]{1,0:T(1,128)} %select_n.46.bias_ref), custom_call_target="tpu_custom_call" | custom-call | flops 3758096384 | bytes 4325376 | tf_op jit(solution)/shard_map/pallas_call | solution.py:70
  220.5 8.5 %all-to-all-start.2 = ((bf16[32,64,256]{2,1,0:T(8,128)(2,1)}), bf16[32,64,256]{2,1,0:T(8,128)(2,1)S(1)}, u32[]{:S(2)}, u32[]{:S(2)}) async-start(bf16[32,64,256]{2,1,0:T(8,128)(2,1)} %bitcast.86), calls=%async_computation.2 | async-start | bytes 2097152 | tf_op jit(solution)/shard_map/all_to_all | solution.py:150
  231.2 22.1 %all-to-all-done.2 = bf16[32,64,256]{2,1,0:T(8,128)(2,1)S(1)} async-done(((bf16[32,64,256]{2,1,0:T(8,128)(2,1)}), bf16[32,64,256]{2,1,0:T(8,128)(2,1)S(1)}, u32[]{:S(2)}, u32[]{:S(2)}) %all-to-all-start.2) | async-done | bytes 1048608 | tf_op jit(solution)/shard_map/all_to_all | solution.py:150
  253.5 1.6 slice_add_fusion
  255.1 1.6 copy.103
  257.6 4.7 %multiply_reduce_fusion = (f32[64]{0:T(128)S(1)}, f32[64,2048]{1,0:T(8,128)S(1)}) fusion(bf16[1024,2048]{1,0:T(8,128)(2,1)} %all-gather.10.cloned.1.call-done, bf16[64,2048]{1,0:T(8,128)(2,1)S(1)} %copy-done.1, f32[8,64,128]{2,1,0:T(8,128)S(1)} %fusion.5, f32[64,8]{0,1:T(8,128)S(1)} %bitcast.90), kind=kOutput, calls=%fused_computation.22 | convolution fusion | flops 1611464704 | bytes 5245184 | tf_op jit(solution)/shard_map/dot_general | solution.py:159
  264.2 63.7 %all_to_all.35 = bf16[64,5,2048]{2,1,0:T(8,128)(2,1)} all-to-all(bf16[64,5,2048]{2,1,0:T(8,128)(2,1)S(1)} %reshape.239), channel_id=1, replica_groups=mesh['dp'=8,'y'=4,'zh'=2,'zl'=4] {'dp','zh','zl'}, dimensions={0} | all-to-all | bytes 2621440 | tf_op jit(solution)/shard_map/all_to_all | solution.py:186
  328.0 2.7 reshape.245
  330.7 8.2 %convolution_bitcast_fusion.1 = f32[4,320,512]{2,1,0:T(8,128)} fusion(bf16[320,2048,1]{1,0,2:T(8,128)(2,1)S(1)} %reshape.245, bf16[4,2048,512]{2,1,0:T(8,128)(2,1)} %all-gather.12.cloned.1.call-done), kind=kOutput, calls=%fused_computation.8 | convolution fusion | flops 2684354560 | bytes 12320768 | tf_op jit(solution)/shard_map/rd,qdf->qrf/dot_general | solution.py:191
  338.9 29.5 %all-gather.14.cloned.1.call-done = bf16[4,256,2048]{2,1,0:T(8,128)(2,1)} async-done(((bf16[1,256,2048]{2,1,0:T(8,128)(2,1)}), bf16[4,256,2048]{2,1,0:T(8,128)(2,1)}) %all-gather.14.cloned.1.call-update) | async-done | bytes 4194320 | tf_op jit(solution)/shard_map/all_gather | solution.py:164
  368.4 4.6 %fusion = bf16[320,2048]{1,0:T(8,128)(2,1)S(1)} fusion(bf16[4,256,2048]{2,1,0:T(8,128)(2,1)} %all-gather.14.cloned.1.call-done, f32[4,320,512]{2,1,0:T(8,128)} %convolution_bitcast_fusion.1), kind=kOutput, calls=%fused_computation.2 | convolution fusion | flops 1344798720 | bytes 8126464 | tf_op jit(solution)/shard_map/qrf,qfd->rd/dot_general | solution.py:193
  373.0 1.6 reshape.241
  374.6 10.8 %all-to-all-start.4 = ((bf16[64,5,2048]{2,1,0:T(8,128)(2,1)}), bf16[64,5,2048]{2,1,0:T(8,128)(2,1)S(1)}, u32[]{:S(2)}, u32[]{:S(2)}) async-start(bf16[64,5,2048]{2,1,0:T(8,128)(2,1)} %reshape.241), calls=%async_computation.4 | async-start | bytes 4194304 | tf_op jit(solution)/shard_map/all_to_all | solution.py:194
  386.0 51.2 %all-to-all-done.4 = bf16[64,5,2048]{2,1,0:T(8,128)(2,1)S(1)} async-done(((bf16[64,5,2048]{2,1,0:T(8,128)(2,1)}), bf16[64,5,2048]{2,1,0:T(8,128)(2,1)S(1)}, u32[]{:S(2)}, u32[]{:S(2)}) %all-to-all-start.4) | async-done | bytes 1310752 | tf_op jit(solution)/shard_map/all_to_all | solution.py:194
  437.8 2.6 fusion.3
  (69 shorter events, 17.2 us)
Async XLA Ops:
  6.5 47.9 %all-gather.8.cloned.1.call-start = ((), (), s32[]{:S(2)}) async-start(), calls=%async_computation.6 | async-start | bytes 1966080 | tf_op jit(solution)/shard_map/all_gather | solution.py:110
  8.3 123.4 %all-gather.6.cloned.1.call-start = ((), (), s32[]{:S(2)}) async-start(), calls=%async_computation.5 | async-start | bytes 2359296 | tf_op jit(solution)/shard_map/all_gather | solution.py:113
  11.3 246.3 %all-gather.10.cloned.1.call-start = ((), (), s32[]{:S(2)}) async-start(), calls=%async_computation.7 | async-start | bytes 4325376 | tf_op jit(solution)/shard_map/all_gather | solution.py:122
  13.0 317.7 %all-gather.12.cloned.1.call-start = ((), (), s32[]{:S(2)}) async-start(), calls=%async_computation.8 | async-start | bytes 10485760 | tf_op jit(solution)/shard_map/all_gather | solution.py:163
  135.0 5.8 %copy-start.2 = (bf16[3,8,128,256]{3,2,1,0:T(8,128)(2,1)S(1)}, bf16[3,8,128,256]{3,2,1,0:T(8,128)(2,1)}, u32[]{:S(2)}) copy-start(bf16[3,8,128,256]{3,2,1,0:T(8,128)(2,1)} %param.15) | copy-start | bytes 4718596
  137.3 18.9 %all-to-all-start = ((bf16[4,8,64,128]{3,2,1,0:T(8,128)(2,1)}), bf16[4,8,64,128]{3,2,1,0:T(8,128)(2,1)S(1)}, u32[]{:S(2)}, u32[]{:S(2)}) async-start(bf16[4,8,64,128]{3,2,1,0:T(8,128)(2,1)} %broadcast_in_dim.20), calls=%async_computation | async-start | bytes 1048576 | tf_op jit(solution)/shard_map/all_to_all | solution.py:135
  142.1 18.1 %copy-start.7 = (s32[1,72]{1,0:T(1,128)S(1)}, s32[1,72]{1,0:T(1,128)}, u32[]{:S(2)}) copy-start(s32[1,72]{1,0:T(1,128)} %param.16) | copy-start | bytes 868
  156.2 46.0 %all-to-all-start.1 = ((bf16[3,32,32,256]{3,2,0,1:T(8,128)(2,1)}), bf16[3,32,32,256]{3,2,0,1:T(8,128)(2,1)S(1)}, u32[]{:S(2)}, u32[]{:S(2)}) async-start(bf16[3,32,32,256]{3,2,0,1:T(8,128)(2,1)} %copy.90), calls=%async_computation.1 | async-start | bytes 3145728 | tf_op jit(solution)/shard_map/all_to_all | solution.py:119
  202.3 1.2 copy-start.3
  220.5 9.1 %copy-start.5 = (s32[64,4]{0,1:T(4,128)S(1)}, s32[64,4]{0,1:T(4,128)}, u32[]{:S(2)}) copy-start(s32[64,4]{0,1:T(4,128)} %param.18) | copy-start | bytes 3076
  220.5 32.8 %all-to-all-start.2 = ((bf16[32,64,256]{2,1,0:T(8,128)(2,1)}), bf16[32,64,256]{2,1,0:T(8,128)(2,1)S(1)}, u32[]{:S(2)}, u32[]{:S(2)}) async-start(bf16[32,64,256]{2,1,0:T(8,128)(2,1)} %bitcast.86), calls=%async_computation.2 | async-start | bytes 2097152 | tf_op jit(solution)/shard_map/all_to_all | solution.py:150
  229.0 139.4 %all-gather.14.cloned.1.call-start = ((), (), s32[]{:S(2)}) async-start(), calls=%async_computation.9 | async-start | bytes 5242880 | tf_op jit(solution)/shard_map/all_gather | solution.py:164
  255.1 2.4 copy-start.1
  257.6 5.5 %copy-start.4 = (f32[2048]{0:T(1024)S(1)}, f32[2048]{0:T(1024)}, u32[]{:S(2)}) copy-start(f32[2048]{0:T(1024)} %param.13) | copy-start | bytes 24580
  262.3 0.8 copy-start
  374.6 10.8 %copy-start.6 = (f32[64,4]{0,1:T(4,128)S(1)}, f32[64,4]{0,1:T(4,128)}, u32[]{:S(2)}) copy-start(f32[64,4]{0,1:T(4,128)} %param.19) | copy-start | bytes 3076
  374.6 62.6 %all-to-all-start.4 = ((bf16[64,5,2048]{2,1,0:T(8,128)(2,1)}), bf16[64,5,2048]{2,1,0:T(8,128)(2,1)S(1)}, u32[]{:S(2)}, u32[]{:S(2)}) async-start(bf16[64,5,2048]{2,1,0:T(8,128)(2,1)} %reshape.241), calls=%async_computation.4 | async-start | bytes 4194304 | tf_op jit(solution)/shard_map/all_to_all | solution.py:194
Sparse Core Ops, SparseCore 0:
  9.2 45.2 all-gather.7
  57.1 74.5 all-gather.5
  134.3 86.0 all-gather.9
  222.1 94.0 all-gather.11
  317.8 50.5 all-gather.13

commit v2 on v1

--- a/solution.py
+++ b/solution.py
@@ -86,6 +86,148 @@
     )(query, cached, fresh, bias)
 
 
+def spread_kernel(
+    w_ref, n_ref, kv_ref, w_out, n_out, kv_out, w_sem, n_sem, kv_send, kv_recv, own_sem
+):
+    n_y, n_zh, n_zl = lax.axis_size("y"), lax.axis_size("zh"), lax.axis_size("zl")
+    y, zh, zl = lax.axis_index("y"), lax.axis_index("zh"), lax.axis_index("zl")
+    group = n_y * n_zh * n_zl
+    me = (y * n_zh + zh) * n_zl + zl
+    slot = y * n_zh + zh
+    over = lax.rem(zh + 1, n_zh)
+    over_slot = y * n_zh + over
+    sub = kv_ref.shape[2] // n_zl
+
+    def at(member):
+        return {"y": member // (n_zh * n_zl), "zh": member // n_zl % n_zh, "zl": member % n_zl}
+
+    def copy(src, dst, send, recv, device):
+        return pltpu.make_async_remote_copy(
+            src_ref=src,
+            dst_ref=dst,
+            send_sem=send,
+            recv_sem=recv,
+            device_id=device,
+            device_id_type=pl.DeviceIdType.MESH,
+        )
+
+    barrier = pltpu.get_barrier_semaphore()
+
+    @pl.loop(1, group)
+    def _(step):
+        pl.semaphore_signal(
+            barrier,
+            inc=1,
+            device_id=at(lax.rem(me + step, group)),
+            device_id_type=pl.DeviceIdType.MESH,
+        )
+
+    pl.semaphore_wait(barrier, group - 1)
+
+    def pages(member):
+        rows = pl.ds(pl.multiple_of(member % n_zl * sub, sub), sub)
+        return kv_ref.at[:, member // n_zl, rows, :]
+
+    own = [
+        pltpu.make_async_copy(w_ref, w_out.at[:, zl], own_sem.at[0]),
+        pltpu.make_async_copy(n_ref, n_out.at[slot], own_sem.at[1]),
+        pltpu.make_async_copy(pages(me), kv_out.at[me], own_sem.at[2]),
+    ]
+    across = copy(n_ref, n_out.at[slot], n_sem.at[0, 0], n_sem.at[1, slot], {"zh": over})
+    across.start()
+    near = []
+    for step in (1, 3, 2):
+        device = {"y": lax.rem(y + step, n_y)}
+        near.append(
+            copy(n_ref, n_out.at[slot], n_sem.at[0, step], n_sem.at[1, slot], device)
+        )
+        near[-1].start()
+    heads = []
+    for step in (1, 3, 2):
+        device = {"zl": lax.rem(zl + step, n_zl)}
+        heads.append(
+            copy(w_ref, w_out.at[:, zl], w_sem.at[0, step], w_sem.at[1, zl], device)
+        )
+        heads[-1].start()
+    for item in own:
+        item.start()
+
+    @pl.loop(1, group)
+    def _(step):
+        to = lax.rem(me + step, group)
+        copy(pages(to), kv_out.at[me], kv_send.at[to], kv_recv.at[me], at(to)).start()
+
+    copy(
+        n_ref, n_out.at[over_slot], n_sem.at[0, 0], n_sem.at[1, over_slot], {"zh": over}
+    ).wait_recv()
+    for step in (1, 3, 2):
+        device = {"y": lax.rem(y + step, n_y)}
+        near.append(
+            copy(
+                n_out.at[over_slot],
+                n_out.at[over_slot],
+                n_sem.at[0, 4 + step],
+                n_sem.at[1, over_slot],
+                device,
+            )
+        )
+        near[-1].start()
+
+    for step in (1, 3, 2):
+        other = lax.rem(y + step, n_y)
+        for half in range(2):
+            there = other * n_zh + half
+            copy(
+                n_ref, n_out.at[there], n_sem.at[0, 0], n_sem.at[1, there], {"y": other}
+            ).wait_recv()
+        there = lax.rem(zl + step, n_zl)
+        copy(
+            w_ref, w_out.at[:, there], w_sem.at[0, 0], w_sem.at[1, there], {"zl": there}
+        ).wait_recv()
+
+    @pl.loop(1, group)
+    def _(step):
+        to = lax.rem(me + step, group)
+        arrival = copy(pages(to), kv_out.at[to], kv_send.at[to], kv_recv.at[to], at(to))
+        arrival.wait_recv()
+        arrival.wait_send()
+
+    across.wait_send()
+    for item in near + heads:
+        item.wait_send()
+    for item in own:
+        item.wait()
+
+
+def spread(sent_w, normed, kv_pool):
+    n_y, n_zh, n_zl = lax.axis_size("y"), lax.axis_size("zh"), lax.axis_size("zl")
+    group = n_y * n_zh * n_zl
+    slots, _, page, lanes = kv_pool.shape
+    kinds, cols, width = sent_w.shape
+    dma = pltpu.SemaphoreType.DMA
+    return pl.pallas_call(
+        spread_kernel,
+        out_shape=(
+            jax.ShapeDtypeStruct((kinds, n_zl, cols, width), jnp.bfloat16),
+            jax.ShapeDtypeStruct((n_y * n_zh,) + normed.shape, jnp.bfloat16),
+            jax.ShapeDtypeStruct((group, slots, page // n_zl, lanes), jnp.bfloat16),
+        ),
+        in_specs=[pl.BlockSpec(memory_space=pltpu.VMEM)] * 3,
+        out_specs=(pl.BlockSpec(memory_space=pl.ANY),) * 3,
+        scratch_shapes=[
+            dma((2, n_zl)),
+            dma((2, n_y * n_zh)),
+            dma((group,)),
+            dma((group,)),
+            dma((3,)),
+        ],
+        compiler_params=pltpu.CompilerParams(collective_id=0, has_side_effects=True),
+        cost_estimate=pl.CostEstimate(
+            flops=0, bytes_accessed=100_000_000, transcendentals=0
+        ),
+    )(sent_w, normed, kv_pool)
+
+
 def local(
     tokens,
     attn_gain,
@@ -107,16 +249,14 @@
     length = cache_len[0]
 
     sent_w = jnp.transpose(w_attn[:3], (0, 2, 1))
-    head_w = lax.all_gather(sent_w, "zl", axis=1, tiled=True)
+    normed = rms_scale(tokens, attn_gain)
+    head_w, piece, arrived = spread(sent_w, normed, kv_pool)
     project_w = head_w.reshape(3 * HD, width)
-    normed = rms_scale(tokens, attn_gain)
-    piece = lax.all_gather(normed, ("y", "zh"), axis=0, tiled=True)
+    piece = piece.reshape(-1, width)
 
     slots = kv_pool.shape[0]
     page = kv_pool.shape[2]
     sub = page // split
-    sent = kv_pool.reshape(slots, HEADS * split, sub, 2 * HD)
-    arrived = lax.all_to_all(sent, GROUP, split_axis=1, concat_axis=0, tiled=True)
     cached = arrived.reshape(group * slots * sub, 2 * HD)
 
     out_w = lax.all_gather(jnp.transpose(w_attn[3], (1, 0)), GROUP, axis=0, tiled=True)

time: 448 us -> 360 us (0.80)
  waiting for transfers between devices: 275 us -> 85.2 us
  Pallas kernels: 17 us -> 125 us
    all_gather x2 -> x0, waiting for transfers between devices: 117 us -> none  [the longest x1 77.3 us: local(): piece = lax.all_gather(normed, ('y', 'zh'), axis=0, tiled=True)]
    pallas_call x0 -> x1, Pallas kernels: none -> 108 us  [spread(): pl.pallas_call(spread_kernel, out_shape=(jax.ShapeDtypeStruct((kinds, n_z...]
    all_to_all x1 -> x0, waiting for transfers between devices: 39.4 us -> none  [local(): lax.all_to_all(sent, GROUP, split_axis=1, concat_axis=0, tiled=True)]
    all_gather x1, waiting for transfers between devices: 29.5 us -> 0.88 us  [local(): down = lax.all_gather(w_down, 'y', axis=0, tiled=True)]
  transfers between devices with their start and end apart: 9 -> 6, of which waited for: 7 -> 4; matrix products, arithmetic and copies ran while one was open for 8% -> 9% of each run, Pallas kernels for 4% -> 35%
where the time goes in v2:
time: 360 us; the launch traced here: 359 us
  Pallas kernels  125 us (35%)
  waiting for transfers between devices  85.2 us (24%)
  blocking collectives  63.8 us (18%)
  starting transfers between devices  25.7 us (7%)
  matrix products  24.4 us (7%)
  between operations  14 us (4%)
  local copies, waits for them, and re-layouts  13.7 us (4%)
  other arithmetic  6.6 us (2%)
    pallas_call x1, Pallas kernels, spread(): pl.pallas_call(spread_kernel, out_shape=(jax.ShapeDtypeStruct((kinds, n_z...  108 us
    all_to_all x1, blocking collectives, local(): lax.all_to_all(buffer.reshape(EXPERTS, cap, width), EXPERT_AXES, split_ax...  63.8 us
    all_to_all x1, waiting for transfers between devices, local(): lax.all_to_all(summed.astype(jnp.bfloat16).reshape(EXPERTS, cap, width),...  51.2 us
    all_to_all x1, waiting for transfers between devices, local(): lax.all_to_all(packed.reshape(group, tok_dev, 2 * HD), GROUP, split_axis=...  21.9 us
    pallas_call x1, Pallas kernels, attend(): pl.pallas_call(attend_kernel, grid=(rows // block,), out_shape=jax.ShapeD...  17.3 us
    all_to_all x1, starting transfers between devices, local(): lax.all_to_all(packed.reshape(group, tok_dev, 2 * HD), GROUP, split_axis=...  10.9 us
    all_to_all x1, starting transfers between devices, local(): lax.all_to_all(summed.astype(jnp.bfloat16).reshape(EXPERTS, cap, width),...  10.8 us
    all_to_all x1, waiting for transfers between devices, local(): query = lax.all_to_all(query, 'zl', split_axis=0, concat_axis=0, tiled=True)  9.75 us
  transfers between devices with their start and end apart: 6, of which 4 were waited for; matrix products, arithmetic and copies ran while one was open for 9% of the time, Pallas kernels for 35%

profile of v2, /device:TPU:1, one launch (start us, length us, event | category | flops | bytes accessed | tf_op | source)
XLA Modules:
  0.0 358.8 jit_solution(677169028664856593)
XLA Ops:
  6.5 1.6 slice_bitcast_fusion.1
  11.4 108.2 %shard_map.109 = (bf16[3,4,32,2048]{3,2,1,0:T(8,128)(2,1)}, bf16[8,64,2048]{2,1,0:T(8,128)(2,1)}, bf16[32,3,32,256]{3,2,1,0:T(8,128)(2,1)}) custom-call(bf16[3,32,2048]{2,1,0:T(8,128)(2,1)} %slice_bitcast_fusion.w_ref, bf16[64,2048]{1,0:T(8,128)(2,1)} %fusion.10.n_ref, bf16[3,8,128,256]{3,2,1,0:T(8,128)(2,1)} %kv_ref.1), custom_call_target="tpu_custom_call" | custom-call | bytes 100000000 | tf_op jit(solution)/shard_map/pallas_call | solution.py:208
  119.7 3.3 fusion.63
  123.0 1.3 fusion.26
  124.4 0.9 broadcast_in_dim.20
  125.4 4.0 %all-to-all-start = ((bf16[4,8,64,128]{3,2,1,0:T(8,128)(2,1)}), bf16[4,8,64,128]{3,2,1,0:T(8,128)(2,1)S(1)}, u32[]{:S(2)}, u32[]{:S(2)}) async-start(bf16[4,8,64,128]{3,2,1,0:T(8,128)(2,1)} %broadcast_in_dim.20), calls=%async_computation | async-start | bytes 1048576 | tf_op jit(solution)/shard_map/all_to_all | solution.py:275
  130.3 0.9 pad_maximum_fusion.new_ref
  131.2 9.8 %all-to-all-done = bf16[4,8,64,128]{3,2,1,0:T(8,128)(2,1)S(1)} async-done(((bf16[4,8,64,128]{3,2,1,0:T(8,128)(2,1)}), bf16[4,8,64,128]{3,2,1,0:T(8,128)(2,1)S(1)}, u32[]{:S(2)}, u32[]{:S(2)}) %all-to-all-start) | async-done | bytes 524320 | tf_op jit(solution)/shard_map/all_to_all | solution.py:275
  140.9 0.8 copy.83
  141.8 17.3 %shard_map.110 = bf16[2048,256]{1,0:T(8,128)(2,1)} custom-call(bf16[2048,128]{1,0:T(8,128)(2,1)} %bitcast.83, bf16[3072,256]{1,0:T(8,128)(2,1)} %bitcast.86, bf16[512,256]{1,0:T(8,128)(2,1)} %pad_maximum_fusion.new_ref, f32[1,3072]{1,0:T(1,128)} %select_n.46.bias_ref), custom_call_target="tpu_custom_call" | custom-call | flops 3758096384 | bytes 4325376 | tf_op jit(solution)/shard_map/pallas_call | solution.py:70
  159.1 10.9 %all-to-all-start.1 = ((bf16[32,64,256]{2,1,0:T(8,128)(2,1)}), bf16[32,64,256]{2,1,0:T(8,128)(2,1)S(1)}, u32[]{:S(2)}, u32[]{:S(2)}) async-start(bf16[32,64,256]{2,1,0:T(8,128)(2,1)} %bitcast.80), calls=%async_computation.1 | async-start | bytes 2097152 | tf_op jit(solution)/shard_map/all_to_all | solution.py:290
  172.3 21.9 %all-to-all-done.1 = bf16[32,64,256]{2,1,0:T(8,128)(2,1)S(1)} async-done(((bf16[32,64,256]{2,1,0:T(8,128)(2,1)}), bf16[32,64,256]{2,1,0:T(8,128)(2,1)S(1)}, u32[]{:S(2)}, u32[]{:S(2)}) %all-to-all-start.1) | async-done | bytes 1048608 | tf_op jit(solution)/shard_map/all_to_all | solution.py:290
  194.4 1.7 slice_add_fusion
  196.1 1.6 copy.96
  198.5 4.8 %multiply_reduce_fusion = (f32[64]{0:T(128)S(1)}, f32[64,2048]{1,0:T(8,128)S(1)}) fusion(bf16[1024,2048]{1,0:T(8,128)(2,1)} %all-gather.4.cloned.1.call-done, bf16[64,2048]{1,0:T(8,128)(2,1)S(1)} %copy-done.1, f32[8,64,128]{2,1,0:T(8,128)S(1)} %fusion.5, f32[64,8]{0,1:T(8,128)S(1)} %bitcast.84), kind=kOutput, calls=%fused_computation.22 | convolution fusion | flops 1611464704 | bytes 5245184 | tf_op jit(solution)/shard_map/dot_general | solution.py:299
  205.2 63.8 %all_to_all.20 = bf16[64,5,2048]{2,1,0:T(8,128)(2,1)} all-to-all(bf16[64,5,2048]{2,1,0:T(8,128)(2,1)S(1)} %reshape.238), channel_id=1, replica_groups=mesh['dp'=8,'y'=4,'zh'=2,'zl'=4] {'dp','zh','zl'}, dimensions={0} | all-to-all | bytes 2621440 | tf_op jit(solution)/shard_map/all_to_all | solution.py:326
  269.0 2.6 reshape.244
  271.6 7.8 %convolution_bitcast_fusion.1 = f32[4,320,512]{2,1,0:T(8,128)} fusion(bf16[320,2048,1]{1,0,2:T(8,128)(2,1)S(1)} %reshape.244, bf16[4,2048,512]{2,1,0:T(8,128)(2,1)} %all-gather.6.cloned.1.call-done), kind=kOutput, calls=%fused_computation.8 | convolution fusion | flops 2684354560 | bytes 12320768 | tf_op jit(solution)/shard_map/rd,qdf->qrf/dot_general | solution.py:331
  279.4 0.9 all-gather.8.cloned.1.call-done
  280.3 4.5 %fusion = bf16[320,2048]{1,0:T(8,128)(2,1)S(1)} fusion(bf16[4,256,2048]{2,1,0:T(8,128)(2,1)} %all-gather.8.cloned.1.call-done, f32[4,320,512]{2,1,0:T(8,128)} %convolution_bitcast_fusion.1), kind=kOutput, calls=%fused_computation.2 | convolution fusion | flops 1344798720 | bytes 8126464 | tf_op jit(solution)/shard_map/qrf,qfd->rd/dot_general | solution.py:333
  284.8 1.6 reshape.240
  286.5 10.8 %all-to-all-start.3 = ((bf16[64,5,2048]{2,1,0:T(8,128)(2,1)}), bf16[64,5,2048]{2,1,0:T(8,128)(2,1)S(1)}, u32[]{:S(2)}, u32[]{:S(2)}) async-start(bf16[64,5,2048]{2,1,0:T(8,128)(2,1)} %reshape.240), calls=%async_computation.3 | async-start | bytes 4194304 | tf_op jit(solution)/shard_map/all_to_all | solution.py:334
  297.9 51.2 %all-to-all-done.3 = bf16[64,5,2048]{2,1,0:T(8,128)(2,1)S(1)} async-done(((bf16[64,5,2048]{2,1,0:T(8,128)(2,1)}), bf16[64,5,2048]{2,1,0:T(8,128)(2,1)S(1)}, u32[]{:S(2)}, u32[]{:S(2)}) %all-to-all-start.3) | async-done | bytes 1310752 | tf_op jit(solution)/shard_map/all_to_all | solution.py:334
  349.7 2.6 fusion.3
  (61 shorter events, 10.1 us)
Async XLA Ops:
  6.5 4.1 %copy-start.2 = (bf16[4,2048,32]{1,2,0:T(8,128)(2,1)S(1)}, bf16[4,2048,32]{1,2,0:T(8,128)(2,1)}, u32[]{:S(2)}) copy-start(bf16[4,2048,32]{1,2,0:T(8,128)(2,1)} %param.14) | copy-start | bytes 1572868
  6.5 3.1 copy-start.1
  6.5 3.2 copy-start.3
  6.5 191.9 %all-gather.4.cloned.1.call-start = ((), (), s32[]{:S(2)}) async-start(), calls=%async_computation.4 | async-start | bytes 4325376 | tf_op jit(solution)/shard_map/all_gather | solution.py:262
  8.2 263.4 %all-gather.6.cloned.1.call-start = ((), (), s32[]{:S(2)}) async-start(), calls=%async_computation.5 | async-start | bytes 10485760 | tf_op jit(solution)/shard_map/all_gather | solution.py:303
  123.0 6.4 %copy-start.7 = (s32[1,72]{1,0:T(1,128)S(1)}, s32[1,72]{1,0:T(1,128)}, u32[]{:S(2)}) copy-start(s32[1,72]{1,0:T(1,128)} %param.16) | copy-start | bytes 868
  125.4 15.6 %all-to-all-start = ((bf16[4,8,64,128]{3,2,1,0:T(8,128)(2,1)}), bf16[4,8,64,128]{3,2,1,0:T(8,128)(2,1)S(1)}, u32[]{:S(2)}, u32[]{:S(2)}) async-start(bf16[4,8,64,128]{3,2,1,0:T(8,128)(2,1)} %broadcast_in_dim.20), calls=%async_computation | async-start | bytes 1048576 | tf_op jit(solution)/shard_map/all_to_all | solution.py:275
  159.1 11.6 %copy-start.5 = (s32[64,4]{0,1:T(4,128)S(1)}, s32[64,4]{0,1:T(4,128)}, u32[]{:S(2)}) copy-start(s32[64,4]{0,1:T(4,128)} %param.18) | copy-start | bytes 3076
  159.1 35.1 %all-to-all-start.1 = ((bf16[32,64,256]{2,1,0:T(8,128)(2,1)}), bf16[32,64,256]{2,1,0:T(8,128)(2,1)S(1)}, u32[]{:S(2)}, u32[]{:S(2)}) async-start(bf16[32,64,256]{2,1,0:T(8,128)(2,1)} %bitcast.80), calls=%async_computation.1 | async-start | bytes 2097152 | tf_op jit(solution)/shard_map/all_to_all | solution.py:290
  169.9 110.4 %all-gather.8.cloned.1.call-start = ((), (), s32[]{:S(2)}) async-start(), calls=%async_computation.6 | async-start | bytes 5242880 | tf_op jit(solution)/shard_map/all_gather | solution.py:304
  198.5 5.6 %copy-start.4 = (f32[2048]{0:T(1024)S(1)}, f32[2048]{0:T(1024)}, u32[]{:S(2)}) copy-start(f32[2048]{0:T(1024)} %param.13) | copy-start | bytes 24580
  203.3 0.8 copy-start
  286.5 10.8 %copy-start.6 = (f32[64,4]{0,1:T(4,128)S(1)}, f32[64,4]{0,1:T(4,128)}, u32[]{:S(2)}) copy-start(f32[64,4]{0,1:T(4,128)} %param.19) | copy-start | bytes 3076
  286.5 62.6 %all-to-all-start.3 = ((bf16[64,5,2048]{2,1,0:T(8,128)(2,1)}), bf16[64,5,2048]{2,1,0:T(8,128)(2,1)S(1)}, u32[]{:S(2)}, u32[]{:S(2)}) async-start(bf16[64,5,2048]{2,1,0:T(8,128)(2,1)} %reshape.240), calls=%async_computation.3 | async-start | bytes 4194304 | tf_op jit(solution)/shard_map/all_to_all | solution.py:334
Sparse Core Ops, SparseCore 0:
  10.0 119.3 all-gather.3
  131.1 95.4 all-gather.5
  228.4 51.8 all-gather.7

commit v3 on v2

--- a/solution.py
+++ b/solution.py
@@ -87,7 +87,18 @@
 
 
 def spread_kernel(
-    w_ref, n_ref, kv_ref, w_out, n_out, kv_out, w_sem, n_sem, kv_send, kv_recv, own_sem
+    w_ref,
+    n_ref,
+    kv_ref,
+    w_out,
+    n_out,
+    kv_out,
+    w_sem,
+    dp_sem,
+    n_sem,
+    kv_send,
+    kv_recv,
+    own_sem,
 ):
     n_y, n_zh, n_zl = lax.axis_size("y"), lax.axis_size("zh"), lax.axis_size("zl")
     y, zh, zl = lax.axis_index("y"), lax.axis_index("zh"), lax.axis_index("zl")
@@ -97,6 +108,11 @@
     over = lax.rem(zh + 1, n_zh)
     over_slot = y * n_zh + over
     sub = kv_ref.shape[2] // n_zl
+    n_dp, dp = lax.axis_size("dp"), lax.axis_index("dp")
+    stripe = w_ref.shape[2]
+
+    def columns(which):
+        return pl.ds(pl.multiple_of(which * stripe, stripe), stripe)
 
     def at(member):
         return {"y": member // (n_zh * n_zl), "zh": member // n_zl % n_zh, "zl": member % n_zl}
@@ -122,14 +138,23 @@
             device_id_type=pl.DeviceIdType.MESH,
         )
 
-    pl.semaphore_wait(barrier, group - 1)
+    @pl.loop(1, n_dp)
+    def _(step):
+        pl.semaphore_signal(
+            barrier,
+            inc=1,
+            device_id={"dp": lax.rem(dp + step, n_dp)},
+            device_id_type=pl.DeviceIdType.MESH,
+        )
+
+    pl.semaphore_wait(barrier, group + n_dp - 2)
 
     def pages(member):
         rows = pl.ds(pl.multiple_of(member % n_zl * sub, sub), sub)
         return kv_ref.at[:, member // n_zl, rows, :]
 
     own = [
-        pltpu.make_async_copy(w_ref, w_out.at[:, zl], own_sem.at[0]),
+        pltpu.make_async_copy(w_ref, w_out.at[:, zl, :, columns(dp)], own_sem.at[0]),
         pltpu.make_async_copy(n_ref, n_out.at[slot], own_sem.at[1]),
         pltpu.make_async_copy(pages(me), kv_out.at[me], own_sem.at[2]),
     ]
@@ -146,7 +171,13 @@
     for step in (1, 3, 2):
         device = {"zl": lax.rem(zl + step, n_zl)}
         heads.append(
-            copy(w_ref, w_out.at[:, zl], w_sem.at[0, step], w_sem.at[1, zl], device)
+            copy(
+                w_ref,
+                w_out.at[:, zl, :, columns(dp)],
+                w_sem.at[0, step],
+                w_sem.at[1, zl],
+                device,
+            )
         )
         heads[-1].start()
     for item in own:
@@ -173,6 +204,30 @@
         )
         near[-1].start()
 
+    own[0].wait()
+    for step in (1, 3, 2):
+        there = lax.rem(zl + step, n_zl)
+        copy(
+            w_ref,
+            w_out.at[:, there, :, columns(dp)],
+            w_sem.at[0, 0],
+            w_sem.at[1, there],
+            {"zl": there},
+        ).wait_recv()
+
+    def stripes(to, which):
+        return copy(
+            w_out.at[:, :, :, columns(which)],
+            w_out.at[:, :, :, columns(which)],
+            dp_sem.at[0, to],
+            dp_sem.at[1, which],
+            {"dp": to},
+        )
+
+    @pl.loop(1, n_dp)
+    def _(step):
+        stripes(lax.rem(dp + step, n_dp), dp).start()
+
     for step in (1, 3, 2):
         other = lax.rem(y + step, n_y)
         for half in range(2):
@@ -180,10 +235,6 @@
             copy(
                 n_ref, n_out.at[there], n_sem.at[0, 0], n_sem.at[1, there], {"y": other}
             ).wait_recv()
-        there = lax.rem(zl + step, n_zl)
-        copy(
-            w_ref, w_out.at[:, there], w_sem.at[0, 0], w_sem.at[1, there], {"zl": there}
-        ).wait_recv()
 
     @pl.loop(1, group)
     def _(step):
@@ -192,10 +243,16 @@
         arrival.wait_recv()
         arrival.wait_send()
 
+    @pl.loop(1, n_dp)
+    def _(step):
+        other = lax.rem(dp + step, n_dp)
+        stripes(other, other).wait_recv()
+        stripes(other, dp).wait_send()
+
     across.wait_send()
     for item in near + heads:
         item.wait_send()
-    for item in own:
+    for item in own[1:]:
         item.wait()
 
 
@@ -203,12 +260,13 @@
     n_y, n_zh, n_zl = lax.axis_size("y"), lax.axis_size("zh"), lax.axis_size("zl")
     group = n_y * n_zh * n_zl
     slots, _, page, lanes = kv_pool.shape
-    kinds, cols, width = sent_w.shape
+    kinds, cols, stripe = sent_w.shape
+    n_dp = lax.axis_size("dp")
     dma = pltpu.SemaphoreType.DMA
     return pl.pallas_call(
         spread_kernel,
         out_shape=(
-            jax.ShapeDtypeStruct((kinds, n_zl, cols, width), jnp.bfloat16),
+            jax.ShapeDtypeStruct((kinds, n_zl, cols, n_dp * stripe), jnp.bfloat16),
             jax.ShapeDtypeStruct((n_y * n_zh,) + normed.shape, jnp.bfloat16),
             jax.ShapeDtypeStruct((group, slots, page // n_zl, lanes), jnp.bfloat16),
         ),
@@ -216,6 +274,7 @@
         out_specs=(pl.BlockSpec(memory_space=pl.ANY),) * 3,
         scratch_shapes=[
             dma((2, n_zl)),
+            dma((2, n_dp)),
             dma((2, n_y * n_zh)),
             dma((group,)),
             dma((group,)),
@@ -226,6 +285,75 @@
             flops=0, bytes_accessed=100_000_000, transcendentals=0
         ),
     )(sent_w, normed, kv_pool)
+
+
+def exchange_kernel(axes, in_ref, out_ref, send, recv, own_sem):
+    sizes = [lax.axis_size(axis) for axis in axes]
+    group = math.prod(sizes)
+    me = 0
+    for axis, size in zip(axes, sizes):
+        me = me * size + lax.axis_index(axis)
+
+    def at(member):
+        device = {}
+        for axis, size in reversed(list(zip(axes, sizes))):
+            device[axis] = member % size
+            member = member // size
+        return device
+
+    barrier = pltpu.get_barrier_semaphore()
+
+    @pl.loop(1, group)
+    def _(step):
+        pl.semaphore_signal(
+            barrier,
+            inc=1,
+            device_id=at(lax.rem(me + step, group)),
+            device_id_type=pl.DeviceIdType.MESH,
+        )
+
+    pl.semaphore_wait(barrier, group - 1)
+    own = pltpu.make_async_copy(in_ref.at[me], out_ref.at[me], own_sem)
+    own.start()
+
+    def copy(to, slot):
+        return pltpu.make_async_remote_copy(
+            src_ref=in_ref.at[to],
+            dst_ref=out_ref.at[slot],
+            send_sem=send.at[to],
+            recv_sem=recv.at[slot],
+            device_id=at(to),
+            device_id_type=pl.DeviceIdType.MESH,
+        )
+
+    @pl.loop(1, group)
+    def _(step):
+        copy(lax.rem(me + step, group), me).start()
+
+    @pl.loop(1, group)
+    def _(step):
+        to = lax.rem(me + step, group)
+        arrival = copy(to, to)
+        arrival.wait_recv()
+        arrival.wait_send()
+
+    own.wait()
+
+
+def exchange(blocks, axes, collective_id):
+    group = blocks.shape[0]
+    dma = pltpu.SemaphoreType.DMA
+    return pl.pallas_call(
+        functools.partial(exchange_kernel, axes),
+        out_shape=jax.ShapeDtypeStruct(blocks.shape, blocks.dtype),
+        in_specs=[pl.BlockSpec(memory_space=pltpu.VMEM)],
+        out_specs=pl.BlockSpec(memory_space=pl.ANY),
+        scratch_shapes=[dma((group,)), dma((group,)), dma],
+        compiler_params=pltpu.CompilerParams(
+            collective_id=collective_id, has_side_effects=True
+        ),
+        cost_estimate=pl.CostEstimate(flops=0, bytes_accessed=60_000_000, transcendentals=0),
+    )(blocks)
 
 
 def local(
@@ -248,7 +376,11 @@
     span = tok_dev * group
     length = cache_len[0]
 
-    sent_w = jnp.transpose(w_attn[:3], (0, 2, 1))
+    n_dp = lax.axis_size("dp")
+    stripe = width // n_dp
+    own_w = lax.dynamic_slice_in_dim(w_attn, lax.axis_index("dp") * stripe, stripe, 1)
+    own_w = jnp.transpose(own_w, (0, 2, 1))
+    sent_w = own_w[:3]
     normed = rms_scale(tokens, attn_gain)
     head_w, piece, arrived = spread(sent_w, normed, kv_pool)
     project_w = head_w.reshape(3 * HD, width)
@@ -259,7 +391,8 @@
     sub = page // split
     cached = arrived.reshape(group * slots * sub, 2 * HD)
 
-    out_w = lax.all_gather(jnp.transpose(w_attn[3], (1, 0)), GROUP, axis=0, tiled=True)
+    out_w = lax.all_gather(own_w[3], GROUP, axis=0, tiled=True)
+    out_w = lax.all_gather(out_w, "dp", axis=0)
 
     place_of = jnp.arange(piece.shape[0], dtype=jnp.int32)
     positions = length + (place_of // tok_dev * split + part) * tok_dev + place_of % tok_dev
@@ -287,16 +420,16 @@
     bias = jnp.where(live, 0.0, very_low).astype(jnp.float32)
 
     packed = attend(query, cached, fresh, bias)
-    landed_rows = lax.all_to_all(
-        packed.reshape(group, tok_dev, 2 * HD), GROUP, split_axis=0, concat_axis=0, tiled=True
-    ).astype(jnp.float32).reshape(HEADS, split, tok_dev, 2 * HD)
+    landed_rows = exchange(packed.reshape(group, tok_dev, 2 * HD), GROUP, 1).astype(jnp.float32).reshape(HEADS, split, tok_dev, 2 * HD)
     tops = landed_rows[..., HD]
     weight = jnp.exp(tops - jnp.max(tops, axis=1, keepdims=True))
     totals = jnp.sum(weight * (landed_rows[..., HD + 1] + landed_rows[..., HD + 2]), axis=1)
     numer = jnp.sum(weight[..., None] * landed_rows[..., :HD], axis=1)
     merged = numer / totals[..., None]
     merged = jnp.transpose(merged, (1, 0, 2)).reshape(tok_dev, HEADS * HD)
-    attn = jnp.dot(merged, out_w.astype(jnp.float32), precision=lax.Precision.HIGHEST)
+    attn = jnp.einsum(
+        "tk,dkn->tdn", merged, out_w.astype(jnp.float32), precision=lax.Precision.HIGHEST
+    ).reshape(tok_dev, width)
     hidden = (tokens.astype(jnp.float32) + attn).astype(jnp.bfloat16)
     normed2 = rms_scale(hidden, ffn_gain)
 
@@ -323,20 +456,16 @@
         token_of.T, place * route_gain.reshape(-1)[:, None], precision=lax.Precision.HIGHEST
     )
     buffer = jnp.dot(dispatch, normed2, preferred_element_type=jnp.float32).astype(jnp.bfloat16)
-    landed = lax.all_to_all(
-        buffer.reshape(EXPERTS, cap, width), EXPERT_AXES, split_axis=0, concat_axis=0, tiled=True
+    landed = exchange(
+        buffer.reshape(EXPERTS, cap, width // HD, HD), EXPERT_AXES, 2
     ).reshape(total_slots, width)
 
     units = w_down.shape[1]
     both = jnp.einsum("rd,qdf->qrf", landed, gate_up, preferred_element_type=jnp.float32)
     activation = (jax.nn.silu(both[..., :units]) * both[..., units:]).astype(jnp.bfloat16)
     summed = jnp.einsum("qrf,qfd->rd", activation, down, preferred_element_type=jnp.float32)
-    output_rows = lax.all_to_all(
-        summed.astype(jnp.bfloat16).reshape(EXPERTS, cap, width),
-        EXPERT_AXES,
-        split_axis=0,
-        concat_axis=0,
-        tiled=True,
+    output_rows = exchange(
+        summed.astype(jnp.bfloat16).reshape(EXPERTS, cap, width // HD, HD), EXPERT_AXES, 3
     ).reshape(total_slots, width)
     moe = jnp.dot(combine, output_rows.astype(jnp.float32), precision=lax.Precision.HIGHEST)
     return (hidden.astype(jnp.float32) + moe).astype(jnp.bfloat16)

time: 360 us -> 330 us (0.917)
  waiting for transfers between devices: 85.2 us -> 11.2 us
  Pallas kernels: 125 us -> 198 us
  starting transfers between devices: 25.7 us -> 3.73 us
  blocking collectives: 63.8 us -> 46.1 us
  local copies, waits for them, and re-layouts: 13.7 us -> 21.6 us
    pallas_call x0 -> x3, Pallas kernels: none -> 111 us  [exchange(): pl.pallas_call(functools.partial(exchange_kernel, axes), out_shape=jax.Sh...]
    all_to_all x2 -> x0, waiting for transfers between devices: 73.1 us -> none  [the longest x1 51.2 us: local(): lax.all_to_all(summed.astype(jnp.bfloat16).reshape(EXPERTS, cap, width),...]
    all_to_all x1 -> x0, blocking collectives: 63.8 us -> none  [local(): lax.all_to_all(buffer.reshape(EXPERTS, cap, width), EXPERT_AXES, split_ax...]
    all_gather x0 -> x1, blocking collectives: none -> 46.1 us  [local(): out_w = lax.all_gather(own_w[3], GROUP, axis=0, tiled=True)]
    pallas_call x1, Pallas kernels: 108 us -> 70.1 us  [spread(): pl.pallas_call(spread_kernel, out_shape=(jax.ShapeDtypeStruct((kinds, n_z...]
    all_to_all x2 -> x0, starting transfers between devices: 21.7 us -> none  [the longest x1 10.9 us: local(): lax.all_to_all(packed.reshape(group, tok_dev, 2 * HD), GROUP, split_axis=...]
    all_gather x0 -> x1, local copies, waits for them, and re-layouts: none -> 6.45 us  [local(): out_w = lax.all_gather(out_w, 'dp', axis=0)]
    unnamed x19 -> x21, local copies, waits for them, and re-layouts: 2.61 us -> 8.88 us
  transfers between devices with their start and end apart: 6 -> 4, of which waited for: 4 -> 1; matrix products, arithmetic and copies ran while one was open for 9% -> 14% of each run, Pallas kernels for 35% -> 47%
where the time goes in v3:
time: 330 us
  Pallas kernels  198 us (60%)
  blocking collectives  46.1 us (14%)
  matrix products  26.3 us (8%)
  local copies, waits for them, and re-layouts  21.6 us (7%)
  between operations  14.1 us (4%)
  waiting for transfers between devices  11.2 us (3%)
  other arithmetic  8.43 us (3%)
  starting transfers between devices  3.73 us (1%)
    pallas_call x3, Pallas kernels, exchange(): pl.pallas_call(functools.partial(exchange_kernel, axes), out_shape=jax.Sh...  111 us
    pallas_call x1, Pallas kernels, spread(): pl.pallas_call(spread_kernel, out_shape=(jax.ShapeDtypeStruct((kinds, n_z...  70.1 us
    all_gather x1, blocking collectives, local(): out_w = lax.all_gather(own_w[3], GROUP, axis=0, tiled=True)  46.1 us
    pallas_call x1, Pallas kernels, attend(): pl.pallas_call(attend_kernel, grid=(rows // block,), out_shape=jax.ShapeD...  17 us
    all_to_all x1, waiting for transfers between devices, local(): query = lax.all_to_all(query, 'zl', split_axis=0, concat_axis=0, tiled=True)  9.77 us
    unnamed x21, local copies, waits for them, and re-layouts  8.88 us
    dot_general x1, matrix products, local(): jnp.einsum('rd,qdf->qrf', landed, gate_up, preferred_element_type=jnp.flo...  7.74 us
  transfers between devices with their start and end apart: 4, of which 1 were waited for; matrix products, arithmetic and copies ran while one was open for 14% of the time, Pallas kernels for 47%

profile of v3, /device:TPU:1, one launch (start us, length us, event | category | flops | bytes accessed | tf_op | source)
XLA Modules:
  0.0 329.5 jit_solution(15725296531642955755)
XLA Ops:
  6.5 1.0 copy-done
  7.6 46.1 %all-gather = bf16[1,1024,256]{2,1,0:T(8,128)(2,1)} all-gather(bf16[1,32,256]{2,1,0:T(8,128)(2,1)S(1)} %slice.77), channel_id=2, replica_groups=mesh['dp'=8,'y'=4,'zh'=2,'zl'=4] {'y','zh','zl'}, dimensions={1}, use_global_device_ids=true | all-gather | bytes 540672 | tf_op jit(solution)/shard_map/all_gather | solution.py:394
  57.5 70.1 %shard_map.109 = (bf16[3,4,32,2048]{3,2,1,0:T(8,128)(2,1)}, bf16[8,64,2048]{2,1,0:T(8,128)(2,1)}, bf16[32,3,32,256]{3,2,1,0:T(8,128)(2,1)}) custom-call(bf16[3,32,256]{2,1,0:T(8,128)(2,1)} %slice.67.w_ref, bf16[64,2048]{1,0:T(8,128)(2,1)} %fusion.14.n_ref, bf16[3,8,128,256]{3,2,1,0:T(8,128)(2,1)} %kv_ref.1), custom_call_target="tpu_custom_call" | custom-call | bytes 100000000 | tf_op jit(solution)/shard_map/pallas_call | solution.py:266
  127.7 3.6 %fusion.68 = f32[512,384]{1,0:T(8,128)S(1)} fusion(bf16[512,2048]{1,0:T(8,128)(2,1)} %bitcast.104, bf16[384,2048]{1,0:T(8,128)(2,1)} %bitcast.106), kind=kOutput, calls=%fused_computation.114 | convolution fusion | flops 805306368 | bytes 4456448 | tf_op jit(solution)/shard_map/dot_general | solution.py:399
  131.3 1.3 fusion.30
  133.7 3.6 %all-to-all-start = ((bf16[4,8,64,128]{3,2,1,0:T(8,128)(2,1)}), bf16[4,8,64,128]{3,2,1,0:T(8,128)(2,1)S(1)}, u32[]{:S(2)}, u32[]{:S(2)}) async-start(bf16[4,8,64,128]{3,2,1,0:T(8,128)(2,1)} %broadcast_in_dim.20), calls=%async_computation | async-start | bytes 1048576 | tf_op jit(solution)/shard_map/all_to_all | solution.py:408
  141.4 9.8 %all-to-all-done = bf16[4,8,64,128]{3,2,1,0:T(8,128)(2,1)S(1)} async-done(((bf16[4,8,64,128]{3,2,1,0:T(8,128)(2,1)}), bf16[4,8,64,128]{3,2,1,0:T(8,128)(2,1)S(1)}, u32[]{:S(2)}, u32[]{:S(2)}) %all-to-all-start) | async-done | bytes 524320 | tf_op jit(solution)/shard_map/all_to_all | solution.py:408
  152.1 17.0 %shard_map.110 = bf16[2048,256]{1,0:T(8,128)(2,1)} custom-call(bf16[2048,128]{1,0:T(8,128)(2,1)} %bitcast.102, bf16[3072,256]{1,0:T(8,128)(2,1)} %bitcast.105, bf16[512,256]{1,0:T(8,128)(2,1)} %pad_maximum_fusion.new_ref, f32[1,3072]{1,0:T(1,128)} %select_n.50.bias_ref), custom_call_target="tpu_custom_call" | custom-call | flops 3758096384 | bytes 4325376 | tf_op jit(solution)/shard_map/pallas_call | solution.py:70
  169.1 29.9 %shard_map.111 = bf16[32,64,256]{2,1,0:T(8,128)(2,1)} custom-call(bf16[32,64,256]{2,1,0:T(8,128)(2,1)} %bitcast.99), custom_call_target="tpu_custom_call" | custom-call | bytes 60000000 | tf_op jit(solution)/shard_map/pallas_call | solution.py:346
  198.9 1.5 bitcast_convert_fusion
  200.4 2.3 fusion.67
  202.7 1.6 copy.65
  204.3 1.6 copy.66
  205.9 1.6 copy.67
  207.9 6.4 %copy.59 = bf16[8,1024,256]{1,2,0:T(8,128)(2,1)} copy(bf16[8,1024,256]{2,1,0:T(8,128)(2,1)} %all-gather.10.cloned.1.call-done) | data formatting | bytes 8388608 | tf_op jit(solution)/shard_map/all_gather | solution.py:395
  214.4 6.2 %multiply_reduce_fusion = (f32[64]{0:T(128)S(1)}, f32[64,2048]{1,0:T(8,128)S(1)}) fusion(bf16[2048,1024]{1,0:T(8,128)(2,1)} %bitcast.94, bf16[64,2048]{1,0:T(8,128)(2,1)S(1)} %copy-done.1, f32[8,64,128]{2,1,0:T(8,128)S(1)} %fusion.9, f32[64,8]{0,1:T(8,128)S(1)} %bitcast.103), kind=kOutput, calls=%fused_computation.25 | convolution fusion | flops 1611464704 | bytes 5245184 | tf_op jit(solution)/shard_map/tk,dkn->tdn/dot_general | solution.py:430
  221.2 1.4 copy.71
  222.7 38.8 %shard_map.112 = bf16[64,5,16,128]{3,2,1,0:T(8,128)(2,1)} custom-call(bf16[64,5,16,128]{3,2,1,0:T(8,128)(2,1)} %bitcast.96), custom_call_target="tpu_custom_call" | custom-call | bytes 60000000 | tf_op jit(solution)/shard_map/pallas_call | solution.py:346
  261.4 2.6 reshape.248
  264.0 7.7 %convolution_bitcast_fusion.1 = f32[4,320,512]{2,1,0:T(8,128)} fusion(bf16[320,2048,1]{1,0,2:T(8,128)(2,1)S(1)} %reshape.248, bf16[4,2048,512]{2,1,0:T(8,128)(2,1)} %all-gather.6.cloned.1.call-done), kind=kOutput, calls=%fused_computation.8 | convolution fusion | flops 2684354560 | bytes 12320768 | tf_op jit(solution)/shard_map/rd,qdf->qrf/dot_general | solution.py:464
  271.8 4.6 %fusion.4 = bf16[40,8,16,128]{3,1,2,0:T(8,128)(2,1)S(1)} fusion(bf16[4,256,2048]{2,1,0:T(8,128)(2,1)} %all-gather.8.cloned.1.call-done, f32[4,320,512]{2,1,0:T(8,128)} %convolution_bitcast_fusion.1), kind=kOutput, calls=%fused_computation.9 | convolution fusion | flops 1344798720 | bytes 8126464 | tf_op jit(solution)/shard_map/qrf,qfd->rd/dot_general | solution.py:466
  276.4 1.4 copy.72
  277.7 42.4 %shard_map.113 = bf16[64,5,16,128]{3,2,1,0:T(8,128)(2,1)} custom-call(bf16[64,5,16,128]{3,2,1,0:T(8,128)(2,1)} %bitcast.97), custom_call_target="tpu_custom_call" | custom-call | bytes 60000000 | tf_op jit(solution)/shard_map/pallas_call | solution.py:346
  320.1 2.9 fusion.3
  (60 shorter events, 10.1 us)
Async XLA Ops:
  6.5 1.0 copy-start
  6.5 201.4 %all-gather.10.cloned.1.call-start = ((), (), s32[]{:S(2)}) async-start(), calls=%async_computation.3 | async-start | bytes 4718592 | tf_op jit(solution)/shard_map/all_gather | solution.py:395
  53.7 2.1 copy-start.1
  53.7 2.9 copy-start.2
  53.7 210.3 %all-gather.6.cloned.1.call-start = ((), (), s32[]{:S(2)}) async-start(), calls=%async_computation.1 | async-start | bytes 10485760 | tf_op jit(solution)/shard_map/all_gather | solution.py:436
  54.5 217.3 %all-gather.8.cloned.1.call-start = ((), (), s32[]{:S(2)}) async-start(), calls=%async_computation.2 | async-start | bytes 5242880 | tf_op jit(solution)/shard_map/all_gather | solution.py:437
  132.6 4.8 %copy-start.4 = (s32[64,4]{0,1:T(4,128)S(1)}, s32[64,4]{0,1:T(4,128)}, u32[]{:S(2)}) copy-start(s32[64,4]{0,1:T(4,128)} %param.18) | copy-start | bytes 3076
  132.6 5.1 %copy-start.6 = (s32[1,72]{1,0:T(1,128)S(1)}, s32[1,72]{1,0:T(1,128)}, u32[]{:S(2)}) copy-start(s32[1,72]{1,0:T(1,128)} %param.16) | copy-start | bytes 868
  132.6 6.9 %copy-start.5 = (f32[64,4]{0,1:T(4,128)S(1)}, f32[64,4]{0,1:T(4,128)}, u32[]{:S(2)}) copy-start(f32[64,4]{0,1:T(4,128)} %param.19) | copy-start | bytes 3076
  133.7 17.5 %all-to-all-start = ((bf16[4,8,64,128]{3,2,1,0:T(8,128)(2,1)}), bf16[4,8,64,128]{3,2,1,0:T(8,128)(2,1)S(1)}, u32[]{:S(2)}, u32[]{:S(2)}) async-start(bf16[4,8,64,128]{3,2,1,0:T(8,128)(2,1)} %broadcast_in_dim.20), calls=%async_computation | async-start | bytes 1048576 | tf_op jit(solution)/shard_map/all_to_all | solution.py:408
  214.4 6.3 %copy-start.3 = (f32[2048]{0:T(1024)S(1)}, f32[2048]{0:T(1024)}, u32[]{:S(2)}) copy-start(f32[2048]{0:T(1024)} %param.13) | copy-start | bytes 24580
Sparse Core Ops, SparseCore 0:
  53.8 46.5 all-gather.9
  102.2 108.1 all-gather.5
  212.3 51.8 all-gather.7

commit v4 on v3

--- a/solution.py
+++ b/solution.py
@@ -90,14 +90,18 @@
     w_ref,
     n_ref,
     kv_ref,
+    o_ref,
     w_out,
     n_out,
     kv_out,
+    o_out,
     w_sem,
     dp_sem,
     n_sem,
     kv_send,
     kv_recv,
+    o_send,
+    o_recv,
     own_sem,
 ):
     n_y, n_zh, n_zl = lax.axis_size("y"), lax.axis_size("zh"), lax.axis_size("zl")
@@ -157,6 +161,7 @@
         pltpu.make_async_copy(w_ref, w_out.at[:, zl, :, columns(dp)], own_sem.at[0]),
         pltpu.make_async_copy(n_ref, n_out.at[slot], own_sem.at[1]),
         pltpu.make_async_copy(pages(me), kv_out.at[me], own_sem.at[2]),
+        pltpu.make_async_copy(o_ref, o_out.at[me], own_sem.at[3]),
     ]
     across = copy(n_ref, n_out.at[slot], n_sem.at[0, 0], n_sem.at[1, slot], {"zh": over})
     across.start()
@@ -187,6 +192,7 @@
     def _(step):
         to = lax.rem(me + step, group)
         copy(pages(to), kv_out.at[me], kv_send.at[to], kv_recv.at[me], at(to)).start()
+        copy(o_ref, o_out.at[me], o_send.at[to], o_recv.at[me], at(to)).start()
 
     copy(
         n_ref, n_out.at[over_slot], n_sem.at[0, 0], n_sem.at[1, over_slot], {"zh": over}
@@ -242,6 +248,9 @@
         arrival = copy(pages(to), kv_out.at[to], kv_send.at[to], kv_recv.at[to], at(to))
         arrival.wait_recv()
         arrival.wait_send()
+        arrival = copy(o_ref, o_out.at[to], o_send.at[to], o_recv.at[to], at(to))
+        arrival.wait_recv()
+        arrival.wait_send()
 
     @pl.loop(1, n_dp)
     def _(step):
@@ -256,7 +265,7 @@
         item.wait()
 
 
-def spread(sent_w, normed, kv_pool):
+def spread(sent_w, normed, kv_pool, sent_o):
     n_y, n_zh, n_zl = lax.axis_size("y"), lax.axis_size("zh"), lax.axis_size("zl")
     group = n_y * n_zh * n_zl
     slots, _, page, lanes = kv_pool.shape
@@ -269,22 +278,25 @@
             jax.ShapeDtypeStruct((kinds, n_zl, cols, n_dp * stripe), jnp.bfloat16),
             jax.ShapeDtypeStruct((n_y * n_zh,) + normed.shape, jnp.bfloat16),
             jax.ShapeDtypeStruct((group, slots, page // n_zl, lanes), jnp.bfloat16),
+            jax.ShapeDtypeStruct((group,) + sent_o.shape, jnp.bfloat16),
         ),
-        in_specs=[pl.BlockSpec(memory_space=pltpu.VMEM)] * 3,
-        out_specs=(pl.BlockSpec(memory_space=pl.ANY),) * 3,
+        in_specs=[pl.BlockSpec(memory_space=pltpu.VMEM)] * 4,
+        out_specs=(pl.BlockSpec(memory_space=pl.ANY),) * 4,
         scratch_shapes=[
             dma((2, n_zl)),
             dma((2, n_dp)),
             dma((2, n_y * n_zh)),
             dma((group,)),
             dma((group,)),
-            dma((3,)),
+            dma((group,)),
+            dma((group,)),
+            dma((4,)),
         ],
         compiler_params=pltpu.CompilerParams(collective_id=0, has_side_effects=True),
         cost_estimate=pl.CostEstimate(
             flops=0, bytes_accessed=100_000_000, transcendentals=0
         ),
-    )(sent_w, normed, kv_pool)
+    )(sent_w, normed, kv_pool, sent_o)
 
 
 def exchange_kernel(axes, in_ref, out_ref, send, recv, own_sem):
@@ -382,7 +394,7 @@
     own_w = jnp.transpose(own_w, (0, 2, 1))
     sent_w = own_w[:3]
     normed = rms_scale(tokens, attn_gain)
-    head_w, piece, arrived = spread(sent_w, normed, kv_pool)
+    head_w, piece, arrived, out_w = spread(sent_w, normed, kv_pool, own_w[3])
     project_w = head_w.reshape(3 * HD, width)
     piece = piece.reshape(-1, width)
 
@@ -391,8 +403,7 @@
     sub = page // split
     cached = arrived.reshape(group * slots * sub, 2 * HD)
 
-    out_w = lax.all_gather(own_w[3], GROUP, axis=0, tiled=True)
-    out_w = lax.all_gather(out_w, "dp", axis=0)
+    gate_up = lax.all_gather(w_gate_up, "y", axis=0, tiled=True)
 
     place_of = jnp.arange(piece.shape[0], dtype=jnp.int32)
     positions = length + (place_of // tok_dev * split + part) * tok_dev + place_of % tok_dev
@@ -420,7 +431,12 @@
     bias = jnp.where(live, 0.0, very_low).astype(jnp.float32)
 
     packed = attend(query, cached, fresh, bias)
-    landed_rows = exchange(packed.reshape(group, tok_dev, 2 * HD), GROUP, 1).astype(jnp.float32).reshape(HEADS, split, tok_dev, 2 * HD)
+    packed, out_w, gate_up = lax.optimization_barrier((packed, out_w, gate_up))
+    out_w = lax.all_gather(out_w.reshape(HEADS * HD, stripe), "dp", axis=0)
+    landed_rows = exchange(packed.reshape(group, tok_dev, 2 * HD), GROUP, 1)
+    landed_rows, w_down = lax.optimization_barrier((landed_rows, w_down))
+    down = lax.all_gather(w_down, "y", axis=0, tiled=True)
+    landed_rows = landed_rows.astype(jnp.float32).reshape(HEADS, split, tok_dev, 2 * HD)
     tops = landed_rows[..., HD]
     weight = jnp.exp(tops - jnp.max(tops, axis=1, keepdims=True))
     totals = jnp.sum(weight * (landed_rows[..., HD + 1] + landed_rows[..., HD + 2]), axis=1)
@@ -428,13 +444,10 @@
     merged = numer / totals[..., None]
     merged = jnp.transpose(merged, (1, 0, 2)).reshape(tok_dev, HEADS * HD)
     attn = jnp.einsum(
-        "tk,dkn->tdn", merged, out_w.astype(jnp.float32), precision=lax.Precision.HIGHEST
+        "tk,dkn->tdn", merged.astype(jnp.bfloat16), out_w, preferred_element_type=jnp.float32
     ).reshape(tok_dev, width)
     hidden = (tokens.astype(jnp.float32) + attn).astype(jnp.bfloat16)
     normed2 = rms_scale(hidden, ffn_gain)
-
-    gate_up = lax.all_gather(w_gate_up, "y", axis=0, tiled=True)
-    down = lax.all_gather(w_down, "y", axis=0, tiled=True)
 
     cap = max(2, tok_dev * TOP * 5 // (4 * EXPERTS))
     flat_expert = routes.reshape(-1)

time: 330 us -> 300 us (0.909)
  blocking collectives: 46.1 us -> 0 us
  waiting for transfers between devices: 11.2 us -> 20.3 us
  Pallas kernels: 198 us -> 207 us
    all_gather x1 -> x0, blocking collectives: 46.1 us -> none  [local(): out_w = lax.all_gather(own_w[3], GROUP, axis=0, tiled=True)]
    all_gather x1, waiting for transfers between devices: 0.02 us -> 10.2 us  [local(): gate_up = lax.all_gather(w_gate_up, 'y', axis=0, tiled=True)]
    pallas_call x1, Pallas kernels: 70.1 us -> 78.1 us  [spread(): pl.pallas_call(spread_kernel, out_shape=(jax.ShapeDtypeStruct((kinds, n_z...]
  transfers between devices with their start and end apart: 4 -> 4, of which waited for: 1 -> 2; matrix products, arithmetic and copies ran while one was open for 14% -> 15% of each run, Pallas kernels for 47% -> 56%
where the time goes in v4:
time: 300 us; the launch traced here: 299 us
  Pallas kernels  207 us (69%)
  matrix products  23.8 us (8%)
  local copies, waits for them, and re-layouts  21.2 us (7%)
  waiting for transfers between devices  20.3 us (7%)
  between operations  14 us (5%)
  other arithmetic  8.44 us (3%)
  starting transfers between devices  3.73 us (1%)
    pallas_call x3, Pallas kernels, exchange(): pl.pallas_call(functools.partial(exchange_kernel, axes), out_shape=jax.Sh...  112 us
    pallas_call x1, Pallas kernels, spread(): pl.pallas_call(spread_kernel, out_shape=(jax.ShapeDtypeStruct((kinds, n_z...  78.1 us
    pallas_call x1, Pallas kernels, attend(): pl.pallas_call(attend_kernel, grid=(rows // block,), out_shape=jax.ShapeD...  17 us
    all_gather x1, waiting for transfers between devices, local(): gate_up = lax.all_gather(w_gate_up, 'y', axis=0, tiled=True)  10.2 us
    all_to_all x1, waiting for transfers between devices, local(): query = lax.all_to_all(query, 'zl', split_axis=0, concat_axis=0, tiled=True)  9.27 us
    unnamed x21, local copies, waits for them, and re-layouts  8.13 us
    dot_general x1, matrix products, local(): jnp.einsum('rd,qdf->qrf', landed, gate_up, preferred_element_type=jnp.flo...  7.74 us
    all_gather x1, local copies, waits for them, and re-layouts, local(): out_w = lax.all_gather(out_w.reshape(HEADS * HD, stripe), 'dp', axis=0)  6.49 us
  transfers between devices with their start and end apart: 4, of which 2 were waited for; matrix products, arithmetic and copies ran while one was open for 15% of the time, Pallas kernels for 56%

profile of v4, /device:TPU:1, one launch (start us, length us, event | category | flops | bytes accessed | tf_op | source)
XLA Modules:
  0.0 298.8 jit_solution(9806607536492332689)
XLA Ops:
  10.5 78.1 %shard_map.109 = (bf16[3,4,32,2048]{3,2,1,0:T(8,128)(2,1)}, bf16[8,64,2048]{2,1,0:T(8,128)(2,1)}, bf16[32,3,32,256]{3,2,1,0:T(8,128)(2,1)}, bf16[32,32,256]{2,1,0:T(8,128)(2,1)}) custom-call(bf16[3,32,256]{2,1,0:T(8,128)(2,1)} %slice.67.w_ref, bf16[64,2048]{1,0:T(8,128)(2,1)} %fusion.14.n_ref, bf16[3,8,128,256]{3,2,1,0:T(8,128)(2,1)} %kv_ref.1, ...), custom_call_target="tpu_custom_call" | custom-call | bytes 100000000 | tf_op jit(solution)/shard_map/pallas_call | solution.py:275
  88.6 3.3 %fusion.68 = f32[512,384]{1,0:T(8,128)S(1)} fusion(bf16[512,2048]{1,0:T(8,128)(2,1)} %bitcast.110, bf16[384,2048]{1,0:T(8,128)(2,1)} %bitcast.112), kind=kOutput, calls=%fused_computation.115 | convolution fusion | flops 805306368 | bytes 4456448 | tf_op jit(solution)/shard_map/dot_general | solution.py:410
  91.9 1.3 fusion.30
  93.3 1.0 broadcast_in_dim.20
  94.3 3.5 %all-to-all-start = ((bf16[4,8,64,128]{3,2,1,0:T(8,128)(2,1)}), bf16[4,8,64,128]{3,2,1,0:T(8,128)(2,1)S(1)}, u32[]{:S(2)}, u32[]{:S(2)}) async-start(bf16[4,8,64,128]{3,2,1,0:T(8,128)(2,1)} %broadcast_in_dim.20), calls=%async_computation | async-start | bytes 1048576 | tf_op jit(solution)/shard_map/all_to_all | solution.py:419
  99.7 9.3 %all-to-all-done = bf16[4,8,64,128]{3,2,1,0:T(8,128)(2,1)S(1)} async-done(((bf16[4,8,64,128]{3,2,1,0:T(8,128)(2,1)}), bf16[4,8,64,128]{3,2,1,0:T(8,128)(2,1)S(1)}, u32[]{:S(2)}, u32[]{:S(2)}) %all-to-all-start) | async-done | bytes 524320 | tf_op jit(solution)/shard_map/all_to_all | solution.py:419
  109.8 17.0 %shard_map.110 = bf16[2048,256]{1,0:T(8,128)(2,1)} custom-call(bf16[2048,128]{1,0:T(8,128)(2,1)} %bitcast.108, bf16[3072,256]{1,0:T(8,128)(2,1)} %bitcast.111, bf16[512,256]{1,0:T(8,128)(2,1)} %pad_maximum_fusion.new_ref, f32[1,3072]{1,0:T(1,128)} %select_n.50.bias_ref), custom_call_target="tpu_custom_call" | custom-call | flops 3758096384 | bytes 4325376 | tf_op jit(solution)/shard_map/pallas_call | solution.py:70
  126.9 10.2 %all-gather.4.cloned.1.call-done = bf16[4,2048,512]{2,1,0:T(8,128)(2,1)} async-done(((bf16[1,2048,512]{2,1,0:T(8,128)(2,1)}), bf16[4,2048,512]{2,1,0:T(8,128)(2,1)}) %all-gather.4.cloned.1.call-update) | async-done | bytes 8388624 | tf_op jit(solution)/shard_map/all_gather | solution.py:406
  137.4 30.0 %shard_map.111 = bf16[32,64,256]{2,1,0:T(8,128)(2,1)} custom-call(bf16[32,64,256]{2,1,0:T(8,128)(2,1)} %bitcast.104), custom_call_target="tpu_custom_call" | custom-call | bytes 60000000 | tf_op jit(solution)/shard_map/pallas_call | solution.py:358
  169.6 1.5 bitcast_convert_fusion
  171.1 2.3 slice_reduce_fusion.1
  173.4 1.6 copy.65
  175.0 1.6 copy.66
  176.6 1.6 copy.67
  178.6 6.5 %copy.59 = bf16[8,1024,256]{1,2,0:T(8,128)(2,1)} copy(bf16[8,1024,256]{2,1,0:T(8,128)(2,1)} %all-gather.6.cloned.1.call-done) | data formatting | bytes 8388608 | tf_op jit(solution)/shard_map/all_gather | solution.py:435
  185.1 4.0 %multiply_reduce_fusion = (f32[64]{0:T(128)S(1)}, f32[64,2048]{1,0:T(8,128)S(1)}) fusion(bf16[2048,1024]{1,0:T(8,128)(2,1)} %bitcast.99, bf16[64,2048]{1,0:T(8,128)(2,1)S(1)} %copy-done.1, f32[64,8]{0,1:T(8,128)S(1)} %bitcast.109, f32[8,64,128]{2,1,0:T(8,128)S(1)} %fusion.9), kind=kOutput, calls=%fused_computation.25 | convolution fusion | flops 269352896 | bytes 5245184 | tf_op jit(solution)/shard_map/tk,dkn->tdn/dot_general | solution.py:446
  189.7 1.4 copy.71
  191.1 42.1 %shard_map.112 = bf16[64,5,16,128]{3,2,1,0:T(8,128)(2,1)} custom-call(bf16[64,5,16,128]{3,2,1,0:T(8,128)(2,1)} %bitcast.101), custom_call_target="tpu_custom_call" | custom-call | bytes 60000000 | tf_op jit(solution)/shard_map/pallas_call | solution.py:358
  233.2 2.4 reshape.244
  235.6 7.7 %convolution_bitcast_fusion.1 = f32[4,320,512]{2,1,0:T(8,128)} fusion(bf16[320,2048,1]{1,0,2:T(8,128)(2,1)S(1)} %reshape.244, bf16[4,2048,512]{2,1,0:T(8,128)(2,1)} %all-gather.4.cloned.1.call-done), kind=kOutput, calls=%fused_computation.8 | convolution fusion | flops 2684354560 | bytes 12320768 | tf_op jit(solution)/shard_map/rd,qdf->qrf/dot_general | solution.py:477
  243.3 4.6 %fusion.4 = bf16[40,8,16,128]{3,1,2,0:T(8,128)(2,1)S(1)} fusion(bf16[4,256,2048]{2,1,0:T(8,128)(2,1)} %all-gather.8.cloned.1.call-done, f32[4,320,512]{2,1,0:T(8,128)} %convolution_bitcast_fusion.1), kind=kOutput, calls=%fused_computation.9 | convolution fusion | flops 1344798720 | bytes 8126464 | tf_op jit(solution)/shard_map/qrf,qfd->rd/dot_general | solution.py:479
  247.9 1.4 copy.72
  249.2 40.1 %shard_map.113 = bf16[64,5,16,128]{3,2,1,0:T(8,128)(2,1)} custom-call(bf16[64,5,16,128]{3,2,1,0:T(8,128)(2,1)} %bitcast.102), custom_call_target="tpu_custom_call" | custom-call | bytes 60000000 | tf_op jit(solution)/shard_map/pallas_call | solution.py:358
  289.3 2.9 fusion.3
  (59 shorter events, 9.5 us)
Async XLA Ops:
  6.5 1.0 copy-start
  6.5 2.3 copy-start.1
  6.5 3.1 %copy-start.2 = (f32[2048]{0:T(1024)S(1)}, f32[2048]{0:T(1024)}, u32[]{:S(2)}) copy-start(f32[2048]{0:T(1024)} %param.12) | copy-start | bytes 24580
  6.5 130.5 %all-gather.4.cloned.1.call-start = ((), (), s32[]{:S(2)}) async-start(), calls=%async_computation.1 | async-start | bytes 10485760 | tf_op jit(solution)/shard_map/all_gather | solution.py:406
  93.2 4.6 %copy-start.6 = (s32[1,72]{1,0:T(1,128)S(1)}, s32[1,72]{1,0:T(1,128)}, u32[]{:S(2)}) copy-start(s32[1,72]{1,0:T(1,128)} %param.16) | copy-start | bytes 868
  94.3 14.7 %all-to-all-start = ((bf16[4,8,64,128]{3,2,1,0:T(8,128)(2,1)}), bf16[4,8,64,128]{3,2,1,0:T(8,128)(2,1)S(1)}, u32[]{:S(2)}, u32[]{:S(2)}) async-start(bf16[4,8,64,128]{3,2,1,0:T(8,128)(2,1)} %broadcast_in_dim.20), calls=%async_computation | async-start | bytes 1048576 | tf_op jit(solution)/shard_map/all_to_all | solution.py:419
  97.8 80.8 %all-gather.6.cloned.1.call-start = ((), (), s32[]{:S(2)}) async-start(), calls=%async_computation.2 | async-start | bytes 4718592 | tf_op jit(solution)/shard_map/all_gather | solution.py:435
  137.1 106.2 %all-gather.8.cloned.1.call-start = ((), (), s32[]{:S(2)}) async-start(), calls=%async_computation.3 | async-start | bytes 5242880 | tf_op jit(solution)/shard_map/all_gather | solution.py:438
  137.3 30.0 %copy-start.4 = (s32[64,4]{0,1:T(4,128)S(1)}, s32[64,4]{0,1:T(4,128)}, u32[]{:S(2)}) copy-start(s32[64,4]{0,1:T(4,128)} %param.18) | copy-start | bytes 3076
  137.4 31.2 %copy-start.5 = (f32[64,4]{0,1:T(4,128)S(1)}, f32[64,4]{0,1:T(4,128)}, u32[]{:S(2)}) copy-start(f32[64,4]{0,1:T(4,128)} %param.19) | copy-start | bytes 3076
  185.1 4.0 %copy-start.3 = (f32[2048]{0:T(1024)S(1)}, f32[2048]{0:T(1024)}, u32[]{:S(2)}) copy-start(f32[2048]{0:T(1024)} %param.13) | copy-start | bytes 24580
Sparse Core Ops, SparseCore 0:
  9.2 127.8 all-gather.3
  138.9 31.5 all-gather.5
  172.3 50.4 all-gather.7

commit v5 on v4

--- a/solution.py
+++ b/solution.py
@@ -443,9 +443,11 @@
     numer = jnp.sum(weight[..., None] * landed_rows[..., :HD], axis=1)
     merged = numer / totals[..., None]
     merged = jnp.transpose(merged, (1, 0, 2)).reshape(tok_dev, HEADS * HD)
-    attn = jnp.einsum(
-        "tk,dkn->tdn", merged.astype(jnp.bfloat16), out_w, preferred_element_type=jnp.float32
-    ).reshape(tok_dev, width)
+    merged = merged.astype(jnp.bfloat16)
+    attn = jnp.concatenate(
+        [jnp.dot(merged, out_w[i], preferred_element_type=jnp.float32) for i in range(n_dp)],
+        axis=1,
+    )
     hidden = (tokens.astype(jnp.float32) + attn).astype(jnp.bfloat16)
     normed2 = rms_scale(hidden, ffn_gain)
 

time: 300 us -> 300 us (level)
  local copies, waits for them, and re-layouts: 21.2 us -> 14.7 us
  matrix products: 23.8 us -> 30 us
    all_gather x1 -> x0, local copies, waits for them, and re-layouts: 6.49 us -> none  [local(): out_w = lax.all_gather(out_w.reshape(HEADS * HD, stripe), 'dp', axis=0)]
    dot_general x1 -> x8, matrix products: 4.01 us -> 10.2 us  [local(): jnp.dot(merged, out_w[i], preferred_element_type=jnp.float32)]
where the time goes in v5:
time: 300 us; the launch traced here: 299 us
  Pallas kernels  207 us (69%)
  matrix products  30 us (10%)
  waiting for transfers between devices  20.3 us (7%)
  local copies, waits for them, and re-layouts  14.7 us (5%)
  between operations  14.1 us (5%)
  other arithmetic  8.77 us (3%)
  starting transfers between devices  3.73 us (1%)
    pallas_call x3, Pallas kernels, exchange(): pl.pallas_call(functools.partial(exchange_kernel, axes), out_shape=jax.Sh...  112 us
    pallas_call x1, Pallas kernels, spread(): pl.pallas_call(spread_kernel, out_shape=(jax.ShapeDtypeStruct((kinds, n_z...  78.1 us
    pallas_call x1, Pallas kernels, attend(): pl.pallas_call(attend_kernel, grid=(rows // block,), out_shape=jax.ShapeD...  17 us
    all_gather x1, waiting for transfers between devices, local(): gate_up = lax.all_gather(w_gate_up, 'y', axis=0, tiled=True)  10.2 us
    dot_general x8, matrix products, local(): jnp.dot(merged, out_w[i], preferred_element_type=jnp.float32)  10.2 us
    all_to_all x1, waiting for transfers between devices, local(): query = lax.all_to_all(query, 'zl', split_axis=0, concat_axis=0, tiled=True)  9.27 us
    unnamed x21, local copies, waits for them, and re-layouts  8.12 us
    dot_general x1, matrix products, local(): jnp.einsum('rd,qdf->qrf', landed, gate_up, preferred_element_type=jnp.flo...  7.74 us
  transfers between devices with their start and end apart: 4, of which 2 were waited for; matrix products, arithmetic and copies ran while one was open for 15% of the time, Pallas kernels for 56%

profile of v5, /device:TPU:1, one launch (start us, length us, event | category | flops | bytes accessed | tf_op | source)
XLA Modules:
  0.0 299.0 jit_solution(18304661017408287193)
XLA Ops:
  10.5 78.1 %shard_map.109 = (bf16[3,4,32,2048]{3,2,1,0:T(8,128)(2,1)}, bf16[8,64,2048]{2,1,0:T(8,128)(2,1)}, bf16[32,3,32,256]{3,2,1,0:T(8,128)(2,1)}, bf16[32,32,256]{2,1,0:T(8,128)(2,1)}) custom-call(bf16[3,32,256]{2,1,0:T(8,128)(2,1)} %slice.99.w_ref, bf16[64,2048]{1,0:T(8,128)(2,1)} %fusion.12.n_ref, bf16[3,8,128,256]{3,2,1,0:T(8,128)(2,1)} %kv_ref.1, ...), custom_call_target="tpu_custom_call" | custom-call | bytes 100000000 | tf_op jit(solution)/shard_map/pallas_call | solution.py:275
  88.6 3.3 %fusion.86 = f32[512,384]{1,0:T(8,128)S(1)} fusion(bf16[512,2048]{1,0:T(8,128)(2,1)} %bitcast.137, bf16[384,2048]{1,0:T(8,128)(2,1)} %bitcast.139), kind=kOutput, calls=%fused_computation.147 | convolution fusion | flops 805306368 | bytes 4456448 | tf_op jit(solution)/shard_map/dot_general | solution.py:410
  91.9 1.3 fusion.32
  94.3 3.5 %all-to-all-start = ((bf16[4,8,64,128]{3,2,1,0:T(8,128)(2,1)}), bf16[4,8,64,128]{3,2,1,0:T(8,128)(2,1)S(1)}, u32[]{:S(2)}, u32[]{:S(2)}) async-start(bf16[4,8,64,128]{3,2,1,0:T(8,128)(2,1)} %broadcast_in_dim.20), calls=%async_computation | async-start | bytes 1048576 | tf_op jit(solution)/shard_map/all_to_all | solution.py:419
  99.7 9.3 %all-to-all-done = bf16[4,8,64,128]{3,2,1,0:T(8,128)(2,1)S(1)} async-done(((bf16[4,8,64,128]{3,2,1,0:T(8,128)(2,1)}), bf16[4,8,64,128]{3,2,1,0:T(8,128)(2,1)S(1)}, u32[]{:S(2)}, u32[]{:S(2)}) %all-to-all-start) | async-done | bytes 524320 | tf_op jit(solution)/shard_map/all_to_all | solution.py:419
  109.8 17.0 %shard_map.110 = bf16[2048,256]{1,0:T(8,128)(2,1)} custom-call(bf16[2048,128]{1,0:T(8,128)(2,1)} %bitcast.135, bf16[3072,256]{1,0:T(8,128)(2,1)} %bitcast.138, bf16[512,256]{1,0:T(8,128)(2,1)} %pad_maximum_fusion.new_ref, f32[1,3072]{1,0:T(1,128)} %select_n.50.bias_ref), custom_call_target="tpu_custom_call" | custom-call | flops 3758096384 | bytes 4325376 | tf_op jit(solution)/shard_map/pallas_call | solution.py:70
  126.9 10.2 %all-gather.4.cloned.1.call-done = bf16[4,2048,512]{2,1,0:T(8,128)(2,1)} async-done(((bf16[1,2048,512]{2,1,0:T(8,128)(2,1)}), bf16[4,2048,512]{2,1,0:T(8,128)(2,1)}) %all-gather.4.cloned.1.call-update) | async-done | bytes 8388624 | tf_op jit(solution)/shard_map/all_gather | solution.py:406
  137.3 30.0 %shard_map.111 = bf16[32,64,256]{2,1,0:T(8,128)(2,1)} custom-call(bf16[32,64,256]{2,1,0:T(8,128)(2,1)} %bitcast.131), custom_call_target="tpu_custom_call" | custom-call | bytes 60000000 | tf_op jit(solution)/shard_map/pallas_call | solution.py:358
  169.6 1.5 bitcast_convert_fusion
  171.0 2.3 slice_reduce_fusion.1
  173.3 1.6 copy.62
  175.0 1.6 copy.63
  176.5 1.6 copy.64
  182.5 1.3 convolution_dynamic-update-slice_fusion.4
  183.8 1.3 convolution_dynamic-update-slice_fusion.3
  186.4 1.3 convolution_dynamic-update-slice_fusion.1
  189.7 1.4 copy.68
  191.2 42.4 %shard_map.112 = bf16[64,5,16,128]{3,2,1,0:T(8,128)(2,1)} custom-call(bf16[64,5,16,128]{3,2,1,0:T(8,128)(2,1)} %bitcast.128), custom_call_target="tpu_custom_call" | custom-call | bytes 60000000 | tf_op jit(solution)/shard_map/pallas_call | solution.py:358
  233.6 2.4 reshape.249
  235.9 7.7 %convolution_bitcast_fusion.1 = f32[4,320,512]{2,1,0:T(8,128)} fusion(bf16[320,2048,1]{1,0,2:T(8,128)(2,1)S(1)} %reshape.249, bf16[4,2048,512]{2,1,0:T(8,128)(2,1)} %all-gather.4.cloned.1.call-done), kind=kOutput, calls=%fused_computation.5 | convolution fusion | flops 2684354560 | bytes 12320768 | tf_op jit(solution)/shard_map/rd,qdf->qrf/dot_general | solution.py:479
  243.7 4.6 %fusion.2 = bf16[40,8,16,128]{3,1,2,0:T(8,128)(2,1)S(1)} fusion(bf16[4,256,2048]{2,1,0:T(8,128)(2,1)} %all-gather.8.cloned.1.call-done, f32[4,320,512]{2,1,0:T(8,128)} %convolution_bitcast_fusion.1), kind=kOutput, calls=%fused_computation.6 | convolution fusion | flops 1344798720 | bytes 8126464 | tf_op jit(solution)/shard_map/qrf,qfd->rd/dot_general | solution.py:481
  248.2 1.4 copy.69
  249.6 39.9 %shard_map.113 = bf16[64,5,16,128]{3,2,1,0:T(8,128)(2,1)} custom-call(bf16[64,5,16,128]{3,2,1,0:T(8,128)(2,1)} %bitcast.129), custom_call_target="tpu_custom_call" | custom-call | bytes 60000000 | tf_op jit(solution)/shard_map/pallas_call | solution.py:358
  289.5 2.9 fusion.1
  (67 shorter events, 17.1 us)
Async XLA Ops:
  6.5 1.0 copy-start
  6.5 2.3 copy-start.1
  6.5 3.1 %copy-start.2 = (f32[2048]{0:T(1024)S(1)}, f32[2048]{0:T(1024)}, u32[]{:S(2)}) copy-start(f32[2048]{0:T(1024)} %param.12) | copy-start | bytes 24580
  6.5 130.5 %all-gather.4.cloned.1.call-start = ((), (), s32[]{:S(2)}) async-start(), calls=%async_computation.1 | async-start | bytes 10485760 | tf_op jit(solution)/shard_map/all_gather | solution.py:406
  91.9 5.9 %copy-start.6 = (s32[1,72]{1,0:T(1,128)S(1)}, s32[1,72]{1,0:T(1,128)}, u32[]{:S(2)}) copy-start(s32[1,72]{1,0:T(1,128)} %param.16) | copy-start | bytes 868
  94.3 14.7 %all-to-all-start = ((bf16[4,8,64,128]{3,2,1,0:T(8,128)(2,1)}), bf16[4,8,64,128]{3,2,1,0:T(8,128)(2,1)S(1)}, u32[]{:S(2)}, u32[]{:S(2)}) async-start(bf16[4,8,64,128]{3,2,1,0:T(8,128)(2,1)} %broadcast_in_dim.20), calls=%async_computation | async-start | bytes 1048576 | tf_op jit(solution)/shard_map/all_to_all | solution.py:419
  97.8 80.9 %all-gather.6.cloned.1.call-start = ((), (), s32[]{:S(2)}) async-start(), calls=%async_computation.2 | async-start | bytes 4718592 | tf_op jit(solution)/shard_map/all_gather | solution.py:435
  126.9 40.5 %copy-start.4 = (s32[64,4]{0,1:T(4,128)S(1)}, s32[64,4]{0,1:T(4,128)}, u32[]{:S(2)}) copy-start(s32[64,4]{0,1:T(4,128)} %param.18) | copy-start | bytes 3076
  126.9 41.7 %copy-start.5 = (f32[64,4]{0,1:T(4,128)S(1)}, f32[64,4]{0,1:T(4,128)}, u32[]{:S(2)}) copy-start(f32[64,4]{0,1:T(4,128)} %param.19) | copy-start | bytes 3076
  137.1 106.6 %all-gather.8.cloned.1.call-start = ((), (), s32[]{:S(2)}) async-start(), calls=%async_computation.3 | async-start | bytes 5242880 | tf_op jit(solution)/shard_map/all_gather | solution.py:438
  183.8 5.4 %copy-start.3 = (f32[2048]{0:T(1024)S(1)}, f32[2048]{0:T(1024)}, u32[]{:S(2)}) copy-start(f32[2048]{0:T(1024)} %param.13) | copy-start | bytes 24580
Sparse Core Ops, SparseCore 0:
  9.2 127.8 all-gather.3
  138.9 31.4 all-gather.5
  172.3 50.5 all-gather.7
